TPU v7x, 32 devices: a whole 2x2x4 slice. The times are simulated.
32 devices in a mesh: dp: 8 (over y, x, core), ctx: 4 (over z).
Axes of the slice: x: 2, y: 2, z: 4, core: 2. Of those that a mesh axis runs over, the one named last changes fastest.
Arguments:
- queries: bfloat16 [16384, 512], P(('dp', 'ctx')), parts along dimension 0, may hold values from -60 to 60
- key_vectors: bfloat16 [16384, 128], P(('dp', 'ctx')), parts along dimension 0, may hold values from -20 to 20
- value_vectors: bfloat16 [16384, 128], P(('dp', 'ctx')), parts along dimension 0, may hold values from -6 to 6
- block_plan: int32 [64], P('dp'), parts along dimension 0, may hold values from 0 to 7, each once
- doc_lengths: int32 [64], P('dp'), parts along dimension 0, may hold values from 1 to 1024, 2048 in all
- out_weight: bfloat16 [512, 4096], P(None, 'ctx'), may hold values from -0.25 to 0.25
Outputs:
- output: bfloat16 [16384, 4096], P(('dp', 'ctx')), parts along dimension 0
There are 8 independent parts, one for each index of `dp`. A program takes and returns all parts, laid end to end along the dimension named above; an argument that names none is the same for every part. Nothing has to cross between parts.
Inputs may be any that keep to these rules, and one draw needn't show every extreme that they name: `doc_lengths`: the 8 lengths sum to 2048.
All inputs are finite; a program needn't handle non-finite values.
Results may differ from a plain program's by a relative error of at most 0.013.
Values may be sent and summed in bfloat16 or wider, within the bound.
No kernel may reach another device: no remote copies, remote signals or barrier semaphores. Data moves between devices by JAX's collectives and lax.ppermute only.
A program may use at most 64 MiB of HBM per device.

v0:
```python
import math

import jax
import jax.numpy as jnp
from jax import lax
from jax.sharding import PartitionSpec as P


def positions(block_plan, first_row, row_count, half_rows):
    row_ids = first_row + jnp.arange(row_count, dtype=jnp.int32)
    block_ids = row_ids // half_rows
    block_table = jnp.arange(block_plan.shape[0], dtype=jnp.int32)
    block_start = jnp.sum(
        jnp.where(block_ids[:, None] == block_table[None, :], block_plan[None, :], 0), axis=1
    )
    return block_start * half_rows + row_ids % half_rows


def document_ids(position, doc_ends):
    return jnp.sum((position[:, None] >= doc_ends[None, :]).astype(jnp.int32), axis=1)


def update(state, query_rows, allowed, key_block, value_block, score_scale):
    row_max, row_total, weighted = state
    scores = (
        jnp.einsum("rgd,kd->grk", query_rows, key_block, preferred_element_type=jnp.float32)
        * score_scale
    )
    scores = jnp.where(allowed[None], scores, jnp.float32(-1e30))
    new_max = jnp.maximum(row_max, jnp.max(scores, axis=2))
    weights = jnp.where(allowed[None], jnp.exp(scores - new_max[:, :, None]), jnp.float32(0.0))
    rescale = jnp.exp(row_max - new_max)
    new_total = row_total * rescale + jnp.sum(weights, axis=2)
    probs = weights.astype(jnp.bfloat16)
    new_weighted = weighted * jnp.transpose(rescale)[:, :, None] + jnp.einsum(
        "grk,kd->rgd", probs, value_block, preferred_element_type=jnp.float32
    )
    return (new_max, new_total, new_weighted)


def shards(queries, key_vectors, value_vectors, block_plan, doc_lengths, out_weight):
    span_rows = queries.shape[0]
    half_rows = span_rows // 2
    head_width = key_vectors.shape[1]
    head_count = queries.shape[1] // head_width
    score_scale = 1.0 / math.sqrt(head_width)
    first_row = lax.axis_index("ctx") * span_rows
    doc_ends = jnp.cumsum(doc_lengths)
    query_pos = positions(block_plan, first_row, span_rows, half_rows)
    query_doc = document_ids(query_pos, doc_ends)
    query_heads = queries.reshape(span_rows, head_count, head_width)
    initial = (
        jnp.full((head_count, span_rows), -1e30, jnp.float32),
        jnp.zeros((head_count, span_rows), jnp.float32),
        jnp.zeros((span_rows, head_count, head_width), jnp.float32),
    )
    key_piece = lax.all_gather(key_vectors, "ctx", axis=0, tiled=True)
    value_piece = lax.all_gather(value_vectors, "ctx", axis=0, tiled=True)
    piece_rows = key_piece.shape[0]
    block_rows = math.gcd(piece_rows, span_rows)

    def one_block(block_index, inner):
        offset = block_index * block_rows
        key_block = lax.dynamic_slice_in_dim(key_piece, offset, block_rows, 0)
        value_block = lax.dynamic_slice_in_dim(value_piece, offset, block_rows, 0)
        key_pos = positions(block_plan, offset, block_rows, half_rows)
        key_doc = document_ids(key_pos, doc_ends)
        allowed = (key_pos[None, :] <= query_pos[:, None]) & (
            key_doc[None, :] == query_doc[:, None]
        )
        results = []
        for half_index in range(2):
            low = half_index * half_rows
            high = low + half_rows
            sub_state = (inner[0][:, low:high], inner[1][:, low:high], inner[2][low:high])
            sub_mask = allowed[low:high]
            sub_query = query_heads[low:high]

            def compute(given, sub_query=sub_query, sub_mask=sub_mask):
                return update(given, sub_query, sub_mask, key_block, value_block, score_scale)

            def keep_state(given):
                return given

            results.append(lax.cond(jnp.any(sub_mask), compute, keep_state, sub_state))
        return (
            jnp.concatenate([results[0][0], results[1][0]], axis=1),
            jnp.concatenate([results[0][1], results[1][1]], axis=1),
            jnp.concatenate([results[0][2], results[1][2]], axis=0),
        )

    row_max, row_total, weighted = lax.fori_loop(0, piece_rows // block_rows, one_block, initial)
    attended = (
        (weighted / jnp.transpose(row_total)[:, :, None])
        .reshape(span_rows, head_count * head_width)
        .astype(jnp.bfloat16)
    )
    return jnp.dot(
        attended,
        lax.all_gather(out_weight, "ctx", axis=1, tiled=True),
        preferred_element_type=jnp.float32,
    ).astype(jnp.bfloat16)


def solution(mesh):
    placed = (
        P(("dp", "ctx"), None),
        P(("dp", "ctx"), None),
        P(("dp", "ctx"), None),
        P("dp"),
        P("dp"),
        P(None, "ctx"),
    )
    return jax.shard_map(
        shards, mesh=mesh, in_specs=placed, out_specs=P(("dp", "ctx"), None), check_vma=False
    )
```

profile of v0, /device:TPU:0, one launch (start us, length us, event | category | flops | bytes accessed | tf_op | source)
XLA Modules:
  0.0 117.2 jit_solution(8152489457986995129)
XLA Ops:
  6.5 0.7 all-gather.2.cloned.1.call-update
  7.3 0.7 select_reduce_fusion.1
  8.0 0.8 reduce-window.8
  8.9 1.3 %copy.16 = bf16[512,512]{0,1:T(8,128)(2,1)S(1)} copy(bf16[512,512]{1,0:T(8,128)(2,1)} %param.12) | data formatting | bytes 1048576 | tf_op args[0]
  10.1 0.3 copy.17
  10.4 22.6 %all_gather.10 = bf16[2048,128]{1,0:T(8,128)(2,1)} all-gather(bf16[512,128]{1,0:T(8,128)(2,1)S(1)} %copy-done), channel_id=1, replica_groups=mesh['dp'=8,'ctx'=4] {'ctx'}, dimensions={0}, use_global_device_ids=true | all-gather | bytes 655360 | tf_op jit(solution)/shard_map/all_gather | solution.py:58
  33.0 22.3 %all_gather.9 = bf16[2048,128]{1,0:T(8,128)(2,1)} all-gather(bf16[512,128]{1,0:T(8,128)(2,1)S(1)} %copy-done.1), channel_id=1, replica_groups=mesh['dp'=8,'ctx'=4] {'ctx'}, dimensions={0}, use_global_device_ids=true | all-gather | bytes 655360 | tf_op jit(solution)/shard_map/all_gather | solution.py:57
  55.4 23.2 %while.19 = (s32[]{:T(128)}, f32[4,512]{1,0:T(4,128)S(1)}, f32[4,512]{1,0:T(4,128)S(1)}, f32[512,4,128]{2,0,1:T(8,128)S(1)}, s32[8]{0:T(128)S(1)}, /*index=5*/s3...) while((s32[]{:T(128)}, f32[4,512]{1,0:T(4,128)S(1)}, ...), condition=%wide.region_16.17_spmd, body=%wide.region_3.16_spmd.sunk | while | flops 552386560 | bytes 22239732 | solution.py:92
  55.5 0.1 select_reduce_fusion.3
  55.6 0.1 convert_reduce_fusion.3
  55.7 0.3 compare_and_fusion.2
  55.9 0.9 slice_reduce_fusion.3
  56.8 1.0 constant_dynamic-slice_fusion.3
  58.5 1.9 %conditional.5 = ((f32[4,256]{1,0:T(4,128)S(1)}, f32[4,256]{1,0:T(4,128)S(1)}, f32[256,4,128]{2,0,1:T(8,128)S(1)})) conditional(s32[]{:T(128)} %convert_element_type.65, (f32[4,256]{1,0:T(4,128)S(1)}, f32[4,256]{1,0:T(4,128)S(1)}, f32[256,4,128]{2,0,1:T(8,128)S(1)}) %tuple.79, (pred[256,512]{0,1:T(8,128)(4,1)S(1)}, ...), branch_computations={%region_7.7_spmd, %region_8.10_spmd} | conditional | flops 275516416 | bytes 8323104 | solution.py:85
  58.6 0.5 fusion
  59.1 0.9 fusion.3
  59.9 0.5 fusion.2
  61.1 1.9 %conditional.4 = ((f32[4,256]{1,0:T(4,128)S(1)}, f32[4,256]{1,0:T(4,128)S(1)}, f32[256,4,128]{2,0,1:T(8,128)S(1)})) conditional(s32[]{:T(128)} %convert_element_type.64, (f32[4,256]{1,0:T(4,128)S(1)}, f32[4,256]{1,0:T(4,128)S(1)}, f32[256,4,128]{2,0,1:T(8,128)S(1)}) %tuple.77, (pred[256,512]{0,1:T(8,128)(4,1)S(1)}, ...), branch_computations={%region_12.12_spmd, %region_13.15_spmd} | conditional | flops 275516416 | bytes 8323104 | solution.py:85
  61.1 0.5 fusion.17
  61.6 0.9 fusion.20
  62.5 0.5 fusion.19
  63.2 0.1 select_reduce_fusion.3
  63.3 0.1 convert_reduce_fusion.3
  63.4 0.3 compare_and_fusion.2
  63.7 0.9 slice_reduce_fusion.3
  64.6 1.0 constant_dynamic-slice_fusion.3
  66.3 1.9 %conditional.5 = ((f32[4,256]{1,0:T(4,128)S(1)}, f32[4,256]{1,0:T(4,128)S(1)}, f32[256,4,128]{2,0,1:T(8,128)S(1)})) conditional(s32[]{:T(128)} %convert_element_type.65, (f32[4,256]{1,0:T(4,128)S(1)}, f32[4,256]{1,0:T(4,128)S(1)}, f32[256,4,128]{2,0,1:T(8,128)S(1)}) %tuple.79, (pred[256,512]{0,1:T(8,128)(4,1)S(1)}, ...), branch_computations={%region_7.7_spmd, %region_8.10_spmd} | conditional | flops 275516416 | bytes 8323104 | solution.py:85
  66.3 0.5 fusion
  66.8 0.9 fusion.3
  67.7 0.5 fusion.2
  69.0 0.1 select_reduce_fusion.3
  69.1 0.1 convert_reduce_fusion.3
  69.2 0.3 compare_and_fusion.2
  69.5 0.9 slice_reduce_fusion.3
  70.4 1.0 constant_dynamic-slice_fusion.3
  72.7 1.9 %conditional.4 = ((f32[4,256]{1,0:T(4,128)S(1)}, f32[4,256]{1,0:T(4,128)S(1)}, f32[256,4,128]{2,0,1:T(8,128)S(1)})) conditional(s32[]{:T(128)} %convert_element_type.64, (f32[4,256]{1,0:T(4,128)S(1)}, f32[4,256]{1,0:T(4,128)S(1)}, f32[256,4,128]{2,0,1:T(8,128)S(1)}) %tuple.77, (pred[256,512]{0,1:T(8,128)(4,1)S(1)}, ...), branch_computations={%region_12.12_spmd, %region_13.15_spmd} | conditional | flops 275516416 | bytes 8323104 | solution.py:85
  72.8 0.5 fusion.17
  73.3 0.9 fusion.20
  74.1 0.5 fusion.19
  74.8 0.1 select_reduce_fusion.3
  74.9 0.1 convert_reduce_fusion.3
  75.0 0.3 compare_and_fusion.2
  75.3 0.9 slice_reduce_fusion.3
  76.2 1.0 constant_dynamic-slice_fusion.3
  78.7 0.3 copy.18
  79.0 0.1 divide_convert_fusion
  79.2 24.7 %all-gather.2.cloned.1.call-done = bf16[512,4096]{1,0:T(8,128)(2,1)} async-done(((bf16[512,1024]{1,0:T(8,128)(2,1)}), bf16[512,4096]{1,0:T(8,128)(2,1)}) %all-gather.2.cloned.1.call-update) | async-done | bytes 4194320 | tf_op jit(solution)/shard_map/all_gather | solution.py:100
  103.8 6.6 %convolution_convert_fusion = bf16[512,4096]{1,0:T(8,128)(2,1)} fusion(bf16[512,512]{0,1:T(8,128)(2,1)S(1)} %bitcast.57, bf16[512,4096]{1,0:T(8,128)(2,1)} %all-gather.2.cloned.1.call-done), kind=kOutput, calls=%fused_computation.64 | convolution fusion | flops 2149580800 | bytes 8912896 | tf_op jit(solution)/shard_map/dot_general | solution.py:98
  (57 shorter events, 1.1 us)
Async XLA Ops:
  6.5 3.9 %copy-start = (bf16[512,128]{1,0:T(8,128)(2,1)S(1)}, bf16[512,128]{1,0:T(8,128)(2,1)}, u32[]{:S(2)}) copy-start(bf16[512,128]{1,0:T(8,128)(2,1)} %param.14) | copy-start | bytes 393220
  6.5 26.5 %copy-start.1 = (bf16[512,128]{1,0:T(8,128)(2,1)S(1)}, bf16[512,128]{1,0:T(8,128)(2,1)}, u32[]{:S(2)}) copy-start(bf16[512,128]{1,0:T(8,128)(2,1)} %param.13) | copy-start | bytes 393220
  6.5 97.3 %all-gather.2.cloned.1.call-start = ((), (), s32[]{:S(2)}) async-start(), calls=%async_computation | async-start | bytes 5242880 | tf_op jit(solution)/shard_map/all_gather | solution.py:100
  8.9 46.6 %copy-start.2 = (s32[8]{0:T(128)S(1)}, s32[8]{0:T(128)}, u32[]{:S(2)}) copy-start(s32[8]{0:T(128)} %param.15) | copy-start | bytes 100
Sparse Core Ops, SparseCore 0:
  8.9 94.8 all-gather.1
where the time goes:
time: 118 us; the launch traced here: 117 us
  blocking collectives  44.8 us (38%)
  waiting for transfers between devices  25.4 us (22%)
  between operations  13.5 us (11%)
  matrix products  12 us (10%)
  other arithmetic  9.81 us (8%)
  local copies, waits for them, and re-layouts  6.21 us (5%)
  loops' own time  5.59 us (5%)
    all_gather x1, waiting for transfers between devices, shards(): lax.all_gather(out_weight, 'ctx', axis=1, tiled=True)  24.7 us
    all_gather x1, blocking collectives, shards(): value_piece = lax.all_gather(value_vectors, 'ctx', axis=0, tiled=True)  22.6 us
    all_gather x1, blocking collectives, shards(): key_piece = lax.all_gather(key_vectors, 'ctx', axis=0, tiled=True)  22.3 us
    dot_general x1, matrix products, shards(): jnp.dot(attended, lax.all_gather(out_weight, 'ctx', axis=1, tiled=True),...  6.57 us
    another operation x1, loops' own time, shards(): lax.fori_loop(0, piece_rows // block_rows, one_block, initial)  5.42 us
    dynamic_slice x4, local copies, waits for them, and re-layouts, one_block(): key_block = lax.dynamic_slice_in_dim(key_piece, offset, block_rows, 0)  3.96 us
    reduce_or x4, other arithmetic, one_block(): results.append(lax.cond(jnp.any(sub_mask), compute, keep_state, sub_state))  3.53 us
    dot_general x4, matrix products, update(): jnp.einsum('grk,kd->rgd', probs, value_block, preferred_element_type=jnp....  3.45 us
  transfers between devices with their start and end apart: 1, of which 1 were waited for; matrix products, arithmetic and copies ran while one was open for 18% of the time, Pallas kernels for 0%

commit v1 on v0

v1 whole, which is shorter than its diff:
```python
import functools
import math

import jax
import jax.numpy as jnp
from jax import lax
from jax.experimental import pallas as pl
from jax.experimental.pallas import tpu as pltpu
from jax.sharding import PartitionSpec as P


NEG = -1e30
MIB = 1 << 20


def order_of(ctx):
    return sorted(range(1, ctx), key=lambda s: (min(s, ctx - s), s))


def doc_start(lengths_ref, position):
    end = jnp.int32(0)
    start = jnp.zeros_like(position)
    for i in range(lengths_ref.shape[0]):
        end = end + lengths_ref[i]
        start = jnp.maximum(start, jnp.where(position >= end, end, 0))
    return start


def scalar_start(lengths_ref, position):
    end = jnp.int32(0)
    start = jnp.int32(0)
    for i in range(lengths_ref.shape[0]):
        end = end + lengths_ref[i]
        start = jnp.maximum(start, jnp.where(position >= end, end, 0))
    return start


def attend_pair(dims, first, diagonal, q_blk, k_blk, start, key_base, q_ref, kv_ref, m_ref, l_ref, acc_ref):
    half, hd, heads, scale = dims
    key = kv_ref[k_blk * half:(k_blk + 1) * half, :hd]
    value_t = kv_ref[k_blk * half:(k_blk + 1) * half, hd:].astype(jnp.float32).T.astype(jnp.bfloat16)
    key_ids = lax.broadcasted_iota(jnp.int32, (half, half), 0)
    keep = key_ids >= start - key_base
    if diagonal:
        keep = keep & (key_ids <= lax.broadcasted_iota(jnp.int32, (half, half), 1))
    bias = jnp.where(keep, jnp.float32(0.0), jnp.float32(NEG))
    for h in range(heads):
        row = q_blk * heads + h
        query = q_ref[q_blk * half:(q_blk + 1) * half, h * hd:(h + 1) * hd]
        s = lax.dot_general(key, query, (((1,), (1,)), ((), ())), preferred_element_type=jnp.float32)
        t = s * scale + bias
        top = jnp.max(t, axis=0, keepdims=True)
        if first:
            m_new = top
        else:
            m_old = m_ref[row:row + 1, :]
            m_new = jnp.maximum(m_old, top)
        p = jnp.exp2(t - m_new)
        total = jnp.sum(p, axis=0, keepdims=True)
        part = jnp.dot(value_t, p.astype(jnp.bfloat16), preferred_element_type=jnp.float32)
        if first:
            l_ref[row:row + 1, :] = total
            acc_ref[row * hd:(row + 1) * hd, :] = part
        else:
            alpha = jnp.exp2(m_old - m_new)
            l_ref[row:row + 1, :] = l_ref[row:row + 1, :] * alpha + total
            acc_ref[row * hd:(row + 1) * hd, :] = acc_ref[row * hd:(row + 1) * hd, :] * alpha + part
        m_ref[row:row + 1, :] = m_new


def attend_chunk(dims, own, me, src, plan_ref, lengths_ref, q_ref, kv_ref, m_ref, l_ref, acc_ref):
    half = dims[0]
    order = [(0, 0), (1, 1), (0, 1), (1, 0)]
    lanes = lax.broadcasted_iota(jnp.int32, (1, half), 1)
    for q_blk, k_blk in order:
        q_base = plan_ref[me * 2 + q_blk] * half
        k_base = plan_ref[src * 2 + k_blk] * half
        args = (q_ref, kv_ref, m_ref, l_ref, acc_ref)
        if own and q_blk == k_blk:
            start = doc_start(lengths_ref, q_base + lanes)
            attend_pair(dims, True, True, q_blk, k_blk, start, k_base, *args)
        else:
            need = (k_base < q_base) & (scalar_start(lengths_ref, q_base) < k_base + half)

            @pl.when(need)
            def _(q_blk=q_blk, k_blk=k_blk, q_base=q_base, k_base=k_base):
                start = doc_start(lengths_ref, q_base + lanes)
                attend_pair(dims, False, False, q_blk, k_blk, start, k_base, *args)


def own_kernel(dims, plan_ref, lengths_ref, q_ref, kv_ref, m_ref, l_ref, acc_ref):
    me = lax.axis_index("ctx")
    attend_chunk(dims, True, me, me, plan_ref, lengths_ref, q_ref, kv_ref, m_ref, l_ref, acc_ref)


def chunk_kernel(dims, ctx, shift, plan_ref, lengths_ref, q_ref, kv_ref, m_in, l_in, acc_in, m_ref, l_ref, acc_ref):
    me = lax.axis_index("ctx")
    src = lax.rem(me + shift, ctx)
    m_ref[...] = m_in[...]
    l_ref[...] = l_in[...]
    acc_ref[...] = acc_in[...]
    attend_chunk(dims, False, me, src, plan_ref, lengths_ref, q_ref, kv_ref, m_ref, l_ref, acc_ref)


def final_kernel(dims, ctx, shift, masks, groups, tile, *refs):
    half, hd, heads, _ = dims
    plan_ref, lengths_ref, q_ref, kv_ref, m_in, l_in, acc_in, w_ref = refs[:8]
    n_groups = len(groups)
    piece_refs = refs[8:8 + 2 * n_groups]
    out_ref, w_buf, att, stage, m_ref, l_ref, acc_ref, w_sem, o_sem = refs[8 + 2 * n_groups:]
    me = lax.axis_index("ctx")
    dp = lax.axis_index("dp")
    piece_rows = piece_refs[0].shape[2]
    cols = w_ref.shape[1]
    loads = {0: [pltpu.make_async_copy(w_ref, w_buf.at[0], w_sem.at[0])]}
    for g, shifts in enumerate(groups):
        for i, s in enumerate(shifts):
            loads[s] = []
            for j, mask in enumerate(masks):
                for core in range(2):
                    row = pl.multiple_of((dp ^ (mask ^ core)) * piece_rows, piece_rows)
                    loads[s].append(
                        pltpu.make_async_copy(
                            piece_refs[2 * g + core].at[j, i],
                            w_buf.at[s, pl.ds(row, piece_rows), :],
                            w_sem.at[s],
                        )
                    )
    slots = list(range(ctx))
    for s in slots:
        for load in loads[s]:
            load.start()
    m_ref[...] = m_in[...]
    l_ref[...] = l_in[...]
    acc_ref[...] = acc_in[...]
    src = lax.rem(me + shift, ctx)
    attend_chunk(dims, False, me, src, plan_ref, lengths_ref, q_ref, kv_ref, m_ref, l_ref, acc_ref)
    for q_blk in range(2):
        for h in range(heads):
            row = q_blk * heads + h
            o = acc_ref[row * hd:(row + 1) * hd, :] / l_ref[row:row + 1, :]
            att[q_blk * half:(q_blk + 1) * half, h * hd:(h + 1) * hd] = o.T.astype(jnp.bfloat16)
    stores = []
    for s in slots:
        for load in loads[s]:
            load.wait()
        base = lax.rem(me + s, ctx) * cols
        for t in range(0, cols, tile):
            y = jnp.dot(att[...], w_buf[s, :, t:t + tile], preferred_element_type=jnp.float32)
            stage[s, :, t:t + tile] = y.astype(jnp.bfloat16)
            store = pltpu.make_async_copy(
                stage.at[s, :, pl.ds(t, tile)],
                out_ref.at[:, pl.ds(pl.multiple_of(base + t, tile), tile)],
                o_sem.at[s, t // tile],
            )
            store.start()
            stores.append(store)
    for store in stores:
        store.wait()


def shards(dp_size, ctx, *args):
    return run(dp_size, ctx, *args)


def run(dp_size, ctx, queries, key_vectors, value_vectors, block_plan, doc_lengths, out_weight):
    rows, width = queries.shape
    hd = key_vectors.shape[1]
    heads = width // hd
    half = rows // 2
    cols = out_weight.shape[1]
    depth = out_weight.shape[0]
    out_cols = cols * ctx
    piece_rows = depth // dp_size
    dims = (half, hd, heads, math.log2(math.e) / math.sqrt(hd))
    near_first = order_of(ctx)
    masks = [b for b in range(0, dp_size, 2)]
    groups = [[s] for s in near_first] if ctx <= 4 else [near_first]

    def from_ctx(x, s):
        return lax.ppermute(x, "ctx", [((i + s) % ctx, i) for i in range(ctx)])

    def from_dp(x, mask):
        return lax.ppermute(x, "dp", [(i ^ mask, i) for i in range(dp_size)])

    piece = lax.dynamic_slice_in_dim(out_weight, lax.axis_index("dp") * piece_rows, piece_rows, 0)
    kv_own = jnp.concatenate([key_vectors, value_vectors], axis=1)
    w_z = {}
    for s in near_first:
        w_z[s] = from_ctx(piece, s)
    kv = {}
    for s in near_first:
        kv[s] = from_ctx(kv_own, s)

    smem = pl.BlockSpec(memory_space=pltpu.SMEM)
    vmem = pl.BlockSpec(memory_space=pltpu.VMEM)
    anyspace = pl.BlockSpec(memory_space=pl.ANY)
    state_shapes = (
        jax.ShapeDtypeStruct((2 * heads, half), jnp.float32),
        jax.ShapeDtypeStruct((2 * heads, half), jnp.float32),
        jax.ShapeDtypeStruct((2 * heads * hd, half), jnp.float32),
    )
    chunk_cost = pl.CostEstimate(
        flops=4 * heads * rows * rows * hd, bytes_accessed=3 * MIB, transcendentals=heads * rows * rows
    )
    state = pl.pallas_call(
        functools.partial(own_kernel, dims),
        out_shape=state_shapes,
        in_specs=[smem, smem, vmem, vmem],
        out_specs=(vmem,) * 3,
        compiler_params=pltpu.CompilerParams(vmem_limit_bytes=16 * MIB),
        cost_estimate=chunk_cost,
        name="attend_own",
    )(block_plan, doc_lengths, queries, kv_own)
    for s in near_first[:-1]:
        state = pl.pallas_call(
            functools.partial(chunk_kernel, dims, ctx, s),
            out_shape=state_shapes,
            in_specs=[smem, smem] + [vmem] * 5,
            out_specs=(vmem,) * 3,
            compiler_params=pltpu.CompilerParams(vmem_limit_bytes=16 * MIB),
            cost_estimate=chunk_cost,
        )(block_plan, doc_lengths, queries, kv[s], *state)

    pieces = []
    for shifts in groups:
        mine = jnp.stack([w_z[s] for s in shifts]) if len(shifts) > 1 else w_z[shifts[0]][None]
        parts = [mine]
        for mask in masks[1:]:
            parts.append(from_dp(mine, mask))
        own = jnp.stack(parts)
        other = from_dp(own, 1)
        pieces += [own, other]

    tile = min(cols, 512)
    last = near_first[-1]
    return pl.pallas_call(
        functools.partial(final_kernel, dims, ctx, last, masks, groups, tile),
        out_shape=jax.ShapeDtypeStruct((rows, out_cols), jnp.bfloat16),
        in_specs=[smem, smem] + [vmem] * 5 + [anyspace] * (1 + len(pieces)),
        out_specs=anyspace,
        scratch_shapes=[
            pltpu.VMEM((ctx, depth, cols), jnp.bfloat16),
            pltpu.VMEM((rows, width), jnp.bfloat16),
            pltpu.VMEM((ctx, rows, cols), jnp.bfloat16),
            pltpu.VMEM((2 * heads, half), jnp.float32),
            pltpu.VMEM((2 * heads, half), jnp.float32),
            pltpu.VMEM((2 * heads * hd, half), jnp.float32),
            pltpu.SemaphoreType.DMA((ctx,)),
            pltpu.SemaphoreType.DMA((ctx, cols // tile)),
        ],
        compiler_params=pltpu.CompilerParams(vmem_limit_bytes=28 * MIB),
        cost_estimate=pl.CostEstimate(
            flops=2 * rows * depth * out_cols, bytes_accessed=8 * MIB, transcendentals=0
        ),
        name="project",
    )(block_plan, doc_lengths, queries, kv[last], *state, out_weight, *pieces)


def solution(mesh):
    placed = (
        P(("dp", "ctx"), None),
        P(("dp", "ctx"), None),
        P(("dp", "ctx"), None),
        P("dp"),
        P("dp"),
        P(None, "ctx"),
    )
    body = functools.partial(shards, mesh.shape["dp"], mesh.shape["ctx"])
    return jax.shard_map(body, mesh=mesh, in_specs=placed, out_specs=P(("dp", "ctx"), None), check_vma=False)
```

time: 118 us -> 63.7 us (0.54)
  blocking collectives: 44.8 us -> 0 us
  starting transfers between devices: 0.01 us -> 31.8 us
  Pallas kernels: 0 us -> 14.6 us
  waiting for transfers between devices: 25.4 us -> 11.1 us
  between operations: 13.5 us -> 0.33 us
  matrix products: 12 us -> 0 us
  other arithmetic: 9.81 us -> 0.2 us
  loops' own time: 5.59 us -> 0 us
    all_gather x2 -> x0, blocking collectives: 44.8 us -> none  [the longest x1 22.6 us: shards(): value_piece = lax.all_gather(value_vectors, 'ctx', axis=0, tiled=True)]
    ppermute x0 -> x18, starting transfers between devices: none -> 31.8 us  [the longest x6 18.5 us: from_ctx(): return lax.ppermute(x, 'ctx', [((i + s) % ctx, i) for i in range(ctx)])]
    all_gather x1 -> x0, waiting for transfers between devices: 24.7 us -> none  [shards(): lax.all_gather(out_weight, 'ctx', axis=1, tiled=True)]
    pallas_call x0 -> x4, Pallas kernels: none -> 14.6 us  [the longest x1 10.1 us: run(): pl.pallas_call(functools.partial(final_kernel, dims, ctx, last, masks, gr...]
    dot_general x9 -> x0, matrix products: 12 us -> none  [the longest x1 6.57 us: shards(): jnp.dot(attended, lax.all_gather(out_weight, 'ctx', axis=1, tiled=True),...]
    ppermute x0 -> x18, waiting for transfers between devices: none -> 11.1 us  [the longest x6 10.9 us: from_ctx(): return lax.ppermute(x, 'ctx', [((i + s) % ctx, i) for i in range(ctx)])]
    another operation x9 -> x0, loops' own time: 5.59 us -> none  [the longest x1 5.42 us: shards(): lax.fori_loop(0, piece_rows // block_rows, one_block, initial)]
    reduce_sum x14 -> x0, other arithmetic: 3.65 us -> none  [the longest x4 2.14 us: update(): new_total = row_total * rescale + jnp.sum(weights, axis=2)]
  transfers between devices with their start and end apart: 1 -> 18, of which waited for: 1 -> 6; matrix products, arithmetic and copies ran while one was open for 18% -> 3% of each run, Pallas kernels for 0% -> 7%
where the time goes in v1:
time: 63.7 us; the launch traced here: 63.3 us
  starting transfers between devices  31.8 us (50%)
  Pallas kernels  14.6 us (23%)
  waiting for transfers between devices  11.1 us (17%)
  local copies, waits for them, and re-layouts  5.15 us (8%)
    ppermute x6, starting transfers between devices, from_ctx(): return lax.ppermute(x, 'ctx', [((i + s) % ctx, i) for i in range(ctx)])  18.5 us
    ppermute x12, starting transfers between devices, from_dp(): return lax.ppermute(x, 'dp', [(i ^ mask, i) for i in range(dp_size)])  13.4 us
    ppermute x6, waiting for transfers between devices, from_ctx(): return lax.ppermute(x, 'ctx', [((i + s) % ctx, i) for i in range(ctx)])  10.9 us
    pallas_call x1, Pallas kernels, run(): pl.pallas_call(functools.partial(final_kernel, dims, ctx, last, masks, gr...  10.1 us
    unnamed x15, local copies, waits for them, and re-layouts  3.3 us
    pallas_call x1, Pallas kernels, run(): pl.pallas_call(functools.partial(own_kernel, dims), out_shape=state_shape...  3.01 us
    pallas_call x2, Pallas kernels, run(): pl.pallas_call(functools.partial(chunk_kernel, dims, ctx, s), out_shape=s...  1.55 us
  transfers between devices with their start and end apart: 18, of which 6 were waited for; matrix products, arithmetic and copies ran while one was open for 3% of the time, Pallas kernels for 7%

profile of v1, /device:TPU:0, one launch (start us, length us, event | category | flops | bytes accessed | tf_op | source)
XLA Modules:
  0.0 63.3 jit_solution(12952003685811231402)
XLA Ops:
  0.0 0.9 %constant_dynamic-slice_fusion = bf16[64,1024]{1,0:T(8,128)(2,1)S(1)} fusion(bf16[512,1024]{1,0:T(8,128)(2,1)} %refs_7_.1, s32[]{:T(128)S(6)} %select_n.3), kind=kLoop, calls=%fused_computation.5 | loop fusion | bytes 262148 | tf_op jit(solution)/shard_map/dynamic_slice | solution.py:186
  0.9 3.1 %collective-permute-start.8 = (bf16[64,1024]{1,0:T(8,128)(2,1)S(1)}, bf16[64,1024]{1,0:T(8,128)(2,1)S(1)}, u32[]{:S(2)}, u32[]{:S(2)}) collective-permute-start(bf16[64,1024]{1,0:T(8,128)(2,1)S(1)} %constant_dynamic-slice_fusion), channel_id=1, source_target_pairs={{3,0},{0,1},{1,2},{2,3},{7,4},{4,5},{5,6},{6,7},{11,8},{8,9},{9,10... | collective-permute-start | bytes 393224 | tf_op jit(solution)/shard_map/ppermute | solution.py:181
  4.0 2.1 %collective-permute-start.3 = (bf16[64,1024]{1,0:T(8,128)(2,1)S(1)}, bf16[64,1024]{1,0:T(8,128)(2,1)S(1)}, u32[]{:S(2)}, u32[]{:S(2)}) collective-permute-start(bf16[64,1024]{1,0:T(8,128)(2,1)S(1)} %constant_dynamic-slice_fusion), channel_id=1, source_target_pairs={{1,0},{2,1},{3,2},{0,3},{5,4},{6,5},{7,6},{4,7},{9,8},{10,9},{11,1... | collective-permute-start | bytes 393224 | tf_op jit(solution)/shard_map/ppermute | solution.py:181
  6.1 0.9 %collective-permute-start.13 = (bf16[64,1024]{1,0:T(8,128)(2,1)S(1)}, bf16[64,1024]{1,0:T(8,128)(2,1)S(1)}, u32[]{:S(2)}, u32[]{:S(2)}) collective-permute-start(bf16[64,1024]{1,0:T(8,128)(2,1)S(1)} %constant_dynamic-slice_fusion), channel_id=1, source_target_pairs={{2,0},{3,1},{0,2},{1,3},{6,4},{7,5},{4,6},{5,7},{10,8},{11,9},{8,1... | collective-permute-start | bytes 393224 | tf_op jit(solution)/shard_map/ppermute | solution.py:181
  7.1 3.3 %collective-permute-done.8 = bf16[64,1024]{1,0:T(8,128)(2,1)S(1)} collective-permute-done((bf16[64,1024]{1,0:T(8,128)(2,1)S(1)}, bf16[64,1024]{1,0:T(8,128)(2,1)S(1)}, u32[]{:S(2)}, u32[]{:S(2)}) %collective-permute-start.8) | collective-permute-done | bytes 131104 | tf_op jit(solution)/shard_map/ppermute | solution.py:181
  10.4 2.7 %collective-permute-start.11 = (bf16[1,64,1024]{2,1,0:T(8,128)(2,1)S(1)}, bf16[1,64,1024]{2,1,0:T(8,128)(2,1)S(1)}, u32[]{:S(2)}, u32[]{:S(2)}) collective-permute-start(bf16[1,64,1024]{2,1,0:T(8,128)(2,1)S(1)} %bitcast.19), channel_id=1, source_target_pairs={{24,0},{28,4},{16,8},{20,12},{8,16},{12,20},{0,24},{4,28},{25,1},{... | collective-permute-start | bytes 393224 | tf_op jit(solution)/shard_map/ppermute | solution.py:184
  13.1 1.2 %collective-permute-start.6 = (bf16[1,64,1024]{2,1,0:T(8,128)(2,1)S(1)}, bf16[1,64,1024]{2,1,0:T(8,128)(2,1)S(1)}, u32[]{:S(2)}, u32[]{:S(2)}) collective-permute-start(bf16[1,64,1024]{2,1,0:T(8,128)(2,1)S(1)} %bitcast.24), channel_id=1, source_target_pairs={{24,0},{28,4},{16,8},{20,12},{8,16},{12,20},{0,24},{4,28},{25,1},{... | collective-permute-start | bytes 393224 | tf_op jit(solution)/shard_map/ppermute | solution.py:184
  14.2 0.8 %collective-permute-start.5 = (bf16[1,64,1024]{2,1,0:T(8,128)(2,1)S(1)}, bf16[1,64,1024]{2,1,0:T(8,128)(2,1)S(1)}, u32[]{:S(2)}, u32[]{:S(2)}) collective-permute-start(bf16[1,64,1024]{2,1,0:T(8,128)(2,1)S(1)} %bitcast.25), channel_id=1, source_target_pairs={{16,0},{20,4},{24,8},{28,12},{0,16},{4,20},{8,24},{12,28},{17,1},{... | collective-permute-start | bytes 393224 | tf_op jit(solution)/shard_map/ppermute | solution.py:184
  15.1 1.5 %collective-permute-start.4 = (bf16[1,64,1024]{2,1,0:T(8,128)(2,1)S(1)}, bf16[1,64,1024]{2,1,0:T(8,128)(2,1)S(1)}, u32[]{:S(2)}, u32[]{:S(2)}) collective-permute-start(bf16[1,64,1024]{2,1,0:T(8,128)(2,1)S(1)} %bitcast.26), channel_id=1, source_target_pairs={{8,0},{12,4},{0,8},{4,12},{24,16},{28,20},{16,24},{20,28},{9,1},{1... | collective-permute-start | bytes 393224 | tf_op jit(solution)/shard_map/ppermute | solution.py:184
  16.6 0.9 %constant_dynamic-update-slice_fusion.1 = bf16[512,256]{1,0:T(8,128)(2,1)S(1)} fusion(bf16[512,128]{1,0:T(8,128)(2,1)} %param.7), kind=kLoop, calls=%fused_computation.4 | loop fusion | bytes 262144
  17.5 0.5 collective-permute-done.13
  18.0 1.5 %collective-permute-start.10 = (bf16[1,64,1024]{2,1,0:T(8,128)(2,1)S(1)}, bf16[1,64,1024]{2,1,0:T(8,128)(2,1)S(1)}, u32[]{:S(2)}, u32[]{:S(2)}) collective-permute-start(bf16[1,64,1024]{2,1,0:T(8,128)(2,1)S(1)} %bitcast.20), channel_id=1, source_target_pairs={{16,0},{20,4},{24,8},{28,12},{0,16},{4,20},{8,24},{12,28},{17,1},{... | collective-permute-start | bytes 393224 | tf_op jit(solution)/shard_map/ppermute | solution.py:184
  19.5 0.0 collective-permute-done.11
  19.5 1.5 %collective-permute-start.9 = (bf16[1,64,1024]{2,1,0:T(8,128)(2,1)S(1)}, bf16[1,64,1024]{2,1,0:T(8,128)(2,1)S(1)}, u32[]{:S(2)}, u32[]{:S(2)}) collective-permute-start(bf16[1,64,1024]{2,1,0:T(8,128)(2,1)S(1)} %bitcast.21), channel_id=1, source_target_pairs={{8,0},{12,4},{0,8},{4,12},{24,16},{28,20},{16,24},{20,28},{9,1},{1... | collective-permute-start | bytes 393224 | tf_op jit(solution)/shard_map/ppermute | solution.py:184
  21.0 0.9 %constant_dynamic-update-slice_fusion.kv_ref = bf16[512,256]{1,0:T(8,128)(2,1)S(1)} fusion(bf16[512,256]{1,0:T(8,128)(2,1)S(1)} %constant_dynamic-update-slice_fusion.1, bf16[512,128]{1,0:T(8,128)(2,1)} %param.8), kind=kLoop, calls=%fused_computation.3 | loop fusion | bytes 262144 | tf_op jit(solution)/shard_map/concatenate | solution.py:187
  21.9 0.9 %collective-permute-start.16 = (bf16[1,64,1024]{2,1,0:T(8,128)(2,1)S(1)}, bf16[1,64,1024]{2,1,0:T(8,128)(2,1)S(1)}, u32[]{:S(2)}, u32[]{:S(2)}) collective-permute-start(bf16[1,64,1024]{2,1,0:T(8,128)(2,1)S(1)} %bitcast.15), channel_id=1, source_target_pairs={{24,0},{28,4},{16,8},{20,12},{8,16},{12,20},{0,24},{4,28},{25,1},{... | collective-permute-start | bytes 393224 | tf_op jit(solution)/shard_map/ppermute | solution.py:184
  22.8 0.0 collective-permute-done.5
  22.8 1.2 %collective-permute-start.15 = (bf16[1,64,1024]{2,1,0:T(8,128)(2,1)S(1)}, bf16[1,64,1024]{2,1,0:T(8,128)(2,1)S(1)}, u32[]{:S(2)}, u32[]{:S(2)}) collective-permute-start(bf16[1,64,1024]{2,1,0:T(8,128)(2,1)S(1)} %bitcast.16), channel_id=1, source_target_pairs={{16,0},{20,4},{24,8},{28,12},{0,16},{4,20},{8,24},{12,28},{17,1},{... | collective-permute-start | bytes 393224 | tf_op jit(solution)/shard_map/ppermute | solution.py:184
  24.0 0.0 collective-permute-done.4
  24.0 1.5 %collective-permute-start.14 = (bf16[1,64,1024]{2,1,0:T(8,128)(2,1)S(1)}, bf16[1,64,1024]{2,1,0:T(8,128)(2,1)S(1)}, u32[]{:S(2)}, u32[]{:S(2)}) collective-permute-start(bf16[1,64,1024]{2,1,0:T(8,128)(2,1)S(1)} %bitcast.17), channel_id=1, source_target_pairs={{8,0},{12,4},{0,8},{4,12},{24,16},{28,20},{16,24},{20,28},{9,1},{1... | collective-permute-start | bytes 393224 | tf_op jit(solution)/shard_map/ppermute | solution.py:184
  25.5 0.1 pad_maximum_fusion.refs_8_
  25.6 0.0 copy-start
  25.6 0.0 copy-start.2
  25.6 0.0 copy-start.4
  25.6 0.0 copy-start.6
  25.6 0.0 collective-permute-done.10
  25.6 3.8 %collective-permute-start.2 = (bf16[512,256]{1,0:T(8,128)(2,1)S(1)}, bf16[512,256]{1,0:T(8,128)(2,1)S(1)}, u32[]{:S(2)}, u32[]{:S(2)}) collective-permute-start(bf16[512,256]{1,0:T(8,128)(2,1)S(1)} %constant_dynamic-update-slice_fusion.kv_ref), channel_id=1, source_target_pairs={{1,0},{2,1},{3,2},{0,3},{5,4},{6,5},{7,6},{4,7},{9,8},{10,9},{11,1... | collective-permute-start | bytes 786440 | tf_op jit(solution)/shard_map/ppermute | solution.py:181
  29.4 0.1 pad_maximum_fusion.1.refs_10_
  29.5 0.0 collective-permute-done.16
  29.5 0.6 collective-permute-start.12
  30.1 0.1 collective-permute-done.15
  30.2 0.1 collective-permute-done.14
  30.3 0.1 pad_maximum_fusion.2.refs_12_
  30.4 0.1 collective-permute-start.17
  30.5 2.8 %collective-permute-start.1 = (bf16[512,256]{1,0:T(8,128)(2,1)S(1)}, bf16[512,256]{1,0:T(8,128)(2,1)S(1)}, u32[]{:S(2)}, u32[]{:S(2)}) collective-permute-start(bf16[512,256]{1,0:T(8,128)(2,1)S(1)} %constant_dynamic-update-slice_fusion.kv_ref), channel_id=1, source_target_pairs={{3,0},{0,1},{1,2},{2,3},{7,4},{4,5},{5,6},{6,7},{11,8},{8,9},{9,10... | collective-permute-start | bytes 786440 | tf_op jit(solution)/shard_map/ppermute | solution.py:181
  33.3 0.9 %collective-permute-done.2.kv_ref = bf16[512,256]{1,0:T(8,128)(2,1)S(1)} collective-permute-done((bf16[512,256]{1,0:T(8,128)(2,1)S(1)}, bf16[512,256]{1,0:T(8,128)(2,1)S(1)}, u32[]{:S(2)}, u32[]{:S(2)}) %collective-permute-start.2) | collective-permute-done | bytes 262176 | tf_op jit(solution)/shard_map/ppermute | solution.py:181
  34.2 5.7 %collective-permute-start = (bf16[512,256]{1,0:T(8,128)(2,1)S(1)}, bf16[512,256]{1,0:T(8,128)(2,1)S(1)}, u32[]{:S(2)}, u32[]{:S(2)}) collective-permute-start(bf16[512,256]{1,0:T(8,128)(2,1)S(1)} %constant_dynamic-update-slice_fusion.kv_ref), channel_id=1, source_target_pairs={{2,0},{3,1},{0,2},{1,3},{6,4},{7,5},{4,6},{5,7},{10,8},{11,9},{8,1... | collective-permute-start | bytes 786440 | tf_op jit(solution)/shard_map/ppermute | solution.py:181
  39.9 1.0 %copy-done.1 = bf16[512,512]{1,0:T(8,128)(2,1)S(1)} copy-done((bf16[512,512]{1,0:T(8,128)(2,1)S(1)}, bf16[512,512]{1,0:T(8,128)(2,1)}, u32[]{:S(2)}) %copy-start.1) | copy-done | bytes 524312
  41.0 0.7 %copy-done.3 = s32[8]{0:T(128)S(1)} copy-done((s32[8]{0:T(128)S(1)}, s32[8]{0:T(128)}, u32[]{:S(2)}) %copy-start.3) | copy-done | bytes 56
  41.6 0.7 %copy-done.5 = s32[8]{0:T(128)S(1)} copy-done((s32[8]{0:T(128)S(1)}, s32[8]{0:T(128)}, u32[]{:S(2)}) %copy-start.5) | copy-done | bytes 56
  42.3 3.0 %attend_own.1 = (f32[8,256]{1,0:T(8,128)S(1)}, f32[8,256]{1,0:T(8,128)S(1)}, f32[1024,256]{1,0:T(8,128)S(1)}) custom-call(s32[8]{0:T(128)S(1)} %copy-done.3, s32[8]{0:T(128)S(1)} %copy-done.5, bf16[512,512]{1,0:T(8,128)(2,1)S(1)} %copy-done.1, bf16[512,256]{1,0:T(8,128)(2,1)S(1)} %constant_dynamic-update-slice_fusion.kv_ref), custom_call_target="tpu_custom_call" | custom-call | flops 536870912 | bytes 3145728 | tf_op jit(solution)/shard_map/attend_own/pallas_call | solution.py:206
  45.3 0.7 %shard_map.64 = (f32[8,256]{1,0:T(8,128)S(1)}, f32[8,256]{1,0:T(8,128)S(1)}, f32[1024,256]{1,0:T(8,128)S(1)}) custom-call(s32[8]{0:T(128)S(1)} %copy-done.3, s32[8]{0:T(128)S(1)} %copy-done.5, bf16[512,512]{1,0:T(8,128)(2,1)S(1)} %copy-done.1, bf16[512,256]{1,0:T(8,128)(2,1)S(1)} %collective-permute-done.2.kv_ref, f32[8,256]{1,0:T(8,128)S(1)} %get-tuple-element.14.m_in, ...), custom_call_target="tpu_custom_call" | custom-call | flops 536870912 | bytes 3145728 | tf_op jit(solution)/shard_map/pallas_call | solution.py:216
  46.0 0.0 collective-permute-done.1.kv_ref
  46.0 0.9 %shard_map.65 = (f32[8,256]{1,0:T(8,128)S(1)}, f32[8,256]{1,0:T(8,128)S(1)}, f32[1024,256]{1,0:T(8,128)S(1)}) custom-call(s32[8]{0:T(128)S(1)} %copy-done.3, s32[8]{0:T(128)S(1)} %copy-done.5, bf16[512,512]{1,0:T(8,128)(2,1)S(1)} %copy-done.1, bf16[512,256]{1,0:T(8,128)(2,1)S(1)} %collective-permute-done.1.kv_ref, f32[8,256]{1,0:T(8,128)S(1)} %get-tuple-element.17.m_in, ...), custom_call_target="tpu_custom_call" | custom-call | flops 536870912 | bytes 3145728 | tf_op jit(solution)/shard_map/pallas_call | solution.py:216
  46.9 6.1 %collective-permute-done.refs_3_ = bf16[512,256]{1,0:T(8,128)(2,1)S(1)} collective-permute-done((bf16[512,256]{1,0:T(8,128)(2,1)S(1)}, bf16[512,256]{1,0:T(8,128)(2,1)S(1)}, u32[]{:S(2)}, u32[]{:S(2)}) %collective-permute-start) | collective-permute-done | bytes 262176 | tf_op jit(solution)/shard_map/ppermute | solution.py:181
  53.0 0.0 collective-permute-done.7.refs_9_
  53.0 0.0 collective-permute-done.12.refs_11_
  53.1 10.1 %project.1 = bf16[512,4096]{1,0:T(8,128)(2,1)} custom-call(s32[8]{0:T(128)S(1)} %copy-done.4, s32[8]{0:T(128)S(1)} %copy-done.6, bf16[512,512]{1,0:T(8,128)(2,1)S(1)} %copy-done.2, bf16[512,256]{1,0:T(8,128)(2,1)S(1)} %collective-permute-done.refs_3_, f32[8,256]{1,0:T(8,128)S(1)} %get-tuple-element.20.refs_4_, f32[8,256]{1,0:T(8,128)S(1)} %get-tuple-element.21.refs_5_, ...), custom_call_target="tpu_custom_call" | custom-call | flops 2147483648 | bytes 8388608 | tf_op jit(solution)/shard_map/project/pallas_call | solution.py:237
  (12 shorter events, 0.0 us)
Async XLA Ops:
  0.9 9.5 %collective-permute-start.8 = (bf16[64,1024]{1,0:T(8,128)(2,1)S(1)}, bf16[64,1024]{1,0:T(8,128)(2,1)S(1)}, u32[]{:S(2)}, u32[]{:S(2)}) collective-permute-start(bf16[64,1024]{1,0:T(8,128)(2,1)S(1)} %constant_dynamic-slice_fusion), channel_id=1, source_target_pairs={{3,0},{0,1},{1,2},{2,3},{7,4},{4,5},{5,6},{6,7},{11,8},{8,9},{9,10... | collective-permute-start | bytes 393224 | tf_op jit(solution)/shard_map/ppermute | solution.py:181
  4.0 9.0 %collective-permute-start.3 = (bf16[64,1024]{1,0:T(8,128)(2,1)S(1)}, bf16[64,1024]{1,0:T(8,128)(2,1)S(1)}, u32[]{:S(2)}, u32[]{:S(2)}) collective-permute-start(bf16[64,1024]{1,0:T(8,128)(2,1)S(1)} %constant_dynamic-slice_fusion), channel_id=1, source_target_pairs={{1,0},{2,1},{3,2},{0,3},{5,4},{6,5},{7,6},{4,7},{9,8},{10,9},{11,1... | collective-permute-start | bytes 393224 | tf_op jit(solution)/shard_map/ppermute | solution.py:181
  6.1 11.9 %collective-permute-start.13 = (bf16[64,1024]{1,0:T(8,128)(2,1)S(1)}, bf16[64,1024]{1,0:T(8,128)(2,1)S(1)}, u32[]{:S(2)}, u32[]{:S(2)}) collective-permute-start(bf16[64,1024]{1,0:T(8,128)(2,1)S(1)} %constant_dynamic-slice_fusion), channel_id=1, source_target_pairs={{2,0},{3,1},{0,2},{1,3},{6,4},{7,5},{4,6},{5,7},{10,8},{11,9},{8,1... | collective-permute-start | bytes 393224 | tf_op jit(solution)/shard_map/ppermute | solution.py:181
  10.4 9.1 %collective-permute-start.11 = (bf16[1,64,1024]{2,1,0:T(8,128)(2,1)S(1)}, bf16[1,64,1024]{2,1,0:T(8,128)(2,1)S(1)}, u32[]{:S(2)}, u32[]{:S(2)}) collective-permute-start(bf16[1,64,1024]{2,1,0:T(8,128)(2,1)S(1)} %bitcast.19), channel_id=1, source_target_pairs={{24,0},{28,4},{16,8},{20,12},{8,16},{12,20},{0,24},{4,28},{25,1},{... | collective-permute-start | bytes 393224 | tf_op jit(solution)/shard_map/ppermute | solution.py:184
  13.1 8.9 %collective-permute-start.6 = (bf16[1,64,1024]{2,1,0:T(8,128)(2,1)S(1)}, bf16[1,64,1024]{2,1,0:T(8,128)(2,1)S(1)}, u32[]{:S(2)}, u32[]{:S(2)}) collective-permute-start(bf16[1,64,1024]{2,1,0:T(8,128)(2,1)S(1)} %bitcast.24), channel_id=1, source_target_pairs={{24,0},{28,4},{16,8},{20,12},{8,16},{12,20},{0,24},{4,28},{25,1},{... | collective-permute-start | bytes 393224 | tf_op jit(solution)/shard_map/ppermute | solution.py:184
  14.2 8.6 %collective-permute-start.5 = (bf16[1,64,1024]{2,1,0:T(8,128)(2,1)S(1)}, bf16[1,64,1024]{2,1,0:T(8,128)(2,1)S(1)}, u32[]{:S(2)}, u32[]{:S(2)}) collective-permute-start(bf16[1,64,1024]{2,1,0:T(8,128)(2,1)S(1)} %bitcast.25), channel_id=1, source_target_pairs={{16,0},{20,4},{24,8},{28,12},{0,16},{4,20},{8,24},{12,28},{17,1},{... | collective-permute-start | bytes 393224 | tf_op jit(solution)/shard_map/ppermute | solution.py:184
  15.1 8.9 %collective-permute-start.4 = (bf16[1,64,1024]{2,1,0:T(8,128)(2,1)S(1)}, bf16[1,64,1024]{2,1,0:T(8,128)(2,1)S(1)}, u32[]{:S(2)}, u32[]{:S(2)}) collective-permute-start(bf16[1,64,1024]{2,1,0:T(8,128)(2,1)S(1)} %bitcast.26), channel_id=1, source_target_pairs={{8,0},{12,4},{0,8},{4,12},{24,16},{28,20},{16,24},{20,28},{9,1},{1... | collective-permute-start | bytes 393224 | tf_op jit(solution)/shard_map/ppermute | solution.py:184
  18.0 7.6 %collective-permute-start.10 = (bf16[1,64,1024]{2,1,0:T(8,128)(2,1)S(1)}, bf16[1,64,1024]{2,1,0:T(8,128)(2,1)S(1)}, u32[]{:S(2)}, u32[]{:S(2)}) collective-permute-start(bf16[1,64,1024]{2,1,0:T(8,128)(2,1)S(1)} %bitcast.20), channel_id=1, source_target_pairs={{16,0},{20,4},{24,8},{28,12},{0,16},{4,20},{8,24},{12,28},{17,1},{... | collective-permute-start | bytes 393224 | tf_op jit(solution)/shard_map/ppermute | solution.py:184
  19.5 9.9 %collective-permute-start.9 = (bf16[1,64,1024]{2,1,0:T(8,128)(2,1)S(1)}, bf16[1,64,1024]{2,1,0:T(8,128)(2,1)S(1)}, u32[]{:S(2)}, u32[]{:S(2)}) collective-permute-start(bf16[1,64,1024]{2,1,0:T(8,128)(2,1)S(1)} %bitcast.21), channel_id=1, source_target_pairs={{8,0},{12,4},{0,8},{4,12},{24,16},{28,20},{16,24},{20,28},{9,1},{1... | collective-permute-start | bytes 393224 | tf_op jit(solution)/shard_map/ppermute | solution.py:184
  21.9 7.6 %collective-permute-start.16 = (bf16[1,64,1024]{2,1,0:T(8,128)(2,1)S(1)}, bf16[1,64,1024]{2,1,0:T(8,128)(2,1)S(1)}, u32[]{:S(2)}, u32[]{:S(2)}) collective-permute-start(bf16[1,64,1024]{2,1,0:T(8,128)(2,1)S(1)} %bitcast.15), channel_id=1, source_target_pairs={{24,0},{28,4},{16,8},{20,12},{8,16},{12,20},{0,24},{4,28},{25,1},{... | collective-permute-start | bytes 393224 | tf_op jit(solution)/shard_map/ppermute | solution.py:184
  22.8 7.3 %collective-permute-start.15 = (bf16[1,64,1024]{2,1,0:T(8,128)(2,1)S(1)}, bf16[1,64,1024]{2,1,0:T(8,128)(2,1)S(1)}, u32[]{:S(2)}, u32[]{:S(2)}) collective-permute-start(bf16[1,64,1024]{2,1,0:T(8,128)(2,1)S(1)} %bitcast.16), channel_id=1, source_target_pairs={{16,0},{20,4},{24,8},{28,12},{0,16},{4,20},{8,24},{12,28},{17,1},{... | collective-permute-start | bytes 393224 | tf_op jit(solution)/shard_map/ppermute | solution.py:184
  24.0 6.3 %collective-permute-start.14 = (bf16[1,64,1024]{2,1,0:T(8,128)(2,1)S(1)}, bf16[1,64,1024]{2,1,0:T(8,128)(2,1)S(1)}, u32[]{:S(2)}, u32[]{:S(2)}) collective-permute-start(bf16[1,64,1024]{2,1,0:T(8,128)(2,1)S(1)} %bitcast.17), channel_id=1, source_target_pairs={{8,0},{12,4},{0,8},{4,12},{24,16},{28,20},{16,24},{20,28},{9,1},{1... | collective-permute-start | bytes 393224 | tf_op jit(solution)/shard_map/ppermute | solution.py:184
  25.6 27.4 %copy-start = (bf16[512,1024]{1,0:T(8,128)(2,1)S(1)}, bf16[512,1024]{1,0:T(8,128)(2,1)}, u32[]{:S(2)}) copy-start(bf16[512,1024]{1,0:T(8,128)(2,1)} %refs_7_.1) | copy-start | bytes 3145732
  25.6 27.4 %copy-start.2 = (bf16[512,512]{1,0:T(8,128)(2,1)S(1)}, bf16[512,512]{1,0:T(8,128)(2,1)}, u32[]{:S(2)}) copy-start(bf16[512,512]{1,0:T(8,128)(2,1)} %refs_2_.1) | copy-start | bytes 1572868
  25.6 27.4 %copy-start.4 = (s32[8]{0:T(128)S(1)}, s32[8]{0:T(128)}, u32[]{:S(2)}) copy-start(s32[8]{0:T(128)} %refs_0_.1) | copy-start | bytes 100
  25.6 27.4 %copy-start.6 = (s32[8]{0:T(128)S(1)}, s32[8]{0:T(128)}, u32[]{:S(2)}) copy-start(s32[8]{0:T(128)} %refs_1_.1) | copy-start | bytes 100
  25.6 8.5 %collective-permute-start.2 = (bf16[512,256]{1,0:T(8,128)(2,1)S(1)}, bf16[512,256]{1,0:T(8,128)(2,1)S(1)}, u32[]{:S(2)}, u32[]{:S(2)}) collective-permute-start(bf16[512,256]{1,0:T(8,128)(2,1)S(1)} %constant_dynamic-update-slice_fusion.kv_ref), channel_id=1, source_target_pairs={{1,0},{2,1},{3,2},{0,3},{5,4},{6,5},{7,6},{4,7},{9,8},{10,9},{11,1... | collective-permute-start | bytes 786440 | tf_op jit(solution)/shard_map/ppermute | solution.py:181
  29.4 23.6 %collective-permute-start.7 = (bf16[4,1,64,1024]{3,2,1,0:T(8,128)(2,1)S(1)}, bf16[4,1,64,1024]{3,2,1,0:T(8,128)(2,1)S(1)}, u32[]{:S(2)}, u32[]{:S(2)}) collective-permute-start(bf16[4,1,64,1024]{3,2,1,0:T(8,128)(2,1)S(1)} %pad_maximum_fusion.refs_8_), channel_id=1, source_target_pairs={{4,0},{0,4},{12,8},{8,12},{20,16},{16,20},{28,24},{24,28},{5,1},{1... | collective-permute-start | bytes 1572872 | tf_op jit(solution)/shard_map/ppermute | solution.py:184
  29.5 23.5 %collective-permute-start.12 = (bf16[4,1,64,1024]{3,2,1,0:T(8,128)(2,1)S(1)}, bf16[4,1,64,1024]{3,2,1,0:T(8,128)(2,1)S(1)}, u32[]{:S(2)}, u32[]{:S(2)}) collective-permute-start(bf16[4,1,64,1024]{3,2,1,0:T(8,128)(2,1)S(1)} %pad_maximum_fusion.1.refs_10_), channel_id=1, source_target_pairs={{4,0},{0,4},{12,8},{8,12},{20,16},{16,20},{28,24},{24,28},{5,1},{1... | collective-permute-start | bytes 1572872 | tf_op jit(solution)/shard_map/ppermute | solution.py:184
  30.4 22.6 %collective-permute-start.17 = (bf16[4,1,64,1024]{3,2,1,0:T(8,128)(2,1)S(1)}, bf16[4,1,64,1024]{3,2,1,0:T(8,128)(2,1)S(1)}, u32[]{:S(2)}, u32[]{:S(2)}) collective-permute-start(bf16[4,1,64,1024]{3,2,1,0:T(8,128)(2,1)S(1)} %pad_maximum_fusion.2.refs_12_), channel_id=1, source_target_pairs={{4,0},{0,4},{12,8},{8,12},{20,16},{16,20},{28,24},{24,28},{5,1},{1... | collective-permute-start | bytes 1572872 | tf_op jit(solution)/shard_map/ppermute | solution.py:184
  30.5 15.5 %collective-permute-start.1 = (bf16[512,256]{1,0:T(8,128)(2,1)S(1)}, bf16[512,256]{1,0:T(8,128)(2,1)S(1)}, u32[]{:S(2)}, u32[]{:S(2)}) collective-permute-start(bf16[512,256]{1,0:T(8,128)(2,1)S(1)} %constant_dynamic-update-slice_fusion.kv_ref), channel_id=1, source_target_pairs={{3,0},{0,1},{1,2},{2,3},{7,4},{4,5},{5,6},{6,7},{11,8},{8,9},{9,10... | collective-permute-start | bytes 786440 | tf_op jit(solution)/shard_map/ppermute | solution.py:181
  34.2 18.8 %collective-permute-start = (bf16[512,256]{1,0:T(8,128)(2,1)S(1)}, bf16[512,256]{1,0:T(8,128)(2,1)S(1)}, u32[]{:S(2)}, u32[]{:S(2)}) collective-permute-start(bf16[512,256]{1,0:T(8,128)(2,1)S(1)} %constant_dynamic-update-slice_fusion.kv_ref), channel_id=1, source_target_pairs={{2,0},{3,1},{0,2},{1,3},{6,4},{7,5},{4,6},{5,7},{10,8},{11,9},{8,1... | collective-permute-start | bytes 786440 | tf_op jit(solution)/shard_map/ppermute | solution.py:181
  39.9 1.0 %copy-start.1 = (bf16[512,512]{1,0:T(8,128)(2,1)S(1)}, bf16[512,512]{1,0:T(8,128)(2,1)}, u32[]{:S(2)}) copy-start(bf16[512,512]{1,0:T(8,128)(2,1)} %refs_2_.1) | copy-start | bytes 1572868
  41.0 0.7 %copy-start.3 = (s32[8]{0:T(128)S(1)}, s32[8]{0:T(128)}, u32[]{:S(2)}) copy-start(s32[8]{0:T(128)} %refs_0_.1) | copy-start | bytes 100
  41.6 0.7 %copy-start.5 = (s32[8]{0:T(128)S(1)}, s32[8]{0:T(128)}, u32[]{:S(2)}) copy-start(s32[8]{0:T(128)} %refs_1_.1) | copy-start | bytes 100

commit v2 on v1

v2 whole, which is shorter than its diff:
```python
import functools
import math

import jax
import jax.numpy as jnp
from jax import lax
from jax.experimental import pallas as pl
from jax.experimental.pallas import tpu as pltpu
from jax.sharding import PartitionSpec as P


NEG = -1e30
MIB = 1 << 20


def doc_start(lengths_ref, position):
    end = jnp.int32(0)
    start = jnp.zeros_like(position)
    for i in range(lengths_ref.shape[0]):
        end = end + lengths_ref[i]
        start = jnp.maximum(start, jnp.where(position >= end, end, 0))
    return start


def scalar_start(lengths_ref, position):
    end = jnp.int32(0)
    start = jnp.int32(0)
    for i in range(lengths_ref.shape[0]):
        end = end + lengths_ref[i]
        start = jnp.maximum(start, jnp.where(position >= end, end, 0))
    return start


def attend_pair(dims, first, diagonal, q_blk, k_blk, start, key_base, q_ref, k_ref, v_ref, m_ref, l_ref, acc_ref):
    half, hd, heads, scale = dims
    key = k_ref[k_blk * half:(k_blk + 1) * half, :]
    value_t = v_ref[k_blk * half:(k_blk + 1) * half, :].astype(jnp.float32).T.astype(jnp.bfloat16)
    key_ids = lax.broadcasted_iota(jnp.int32, (half, half), 0)
    keep = key_ids >= start - key_base
    if diagonal:
        keep = keep & (key_ids <= lax.broadcasted_iota(jnp.int32, (half, half), 1))
    bias = jnp.where(keep, jnp.float32(0.0), jnp.float32(NEG))
    for h in range(heads):
        row = q_blk * heads + h
        query = q_ref[q_blk * half:(q_blk + 1) * half, h * hd:(h + 1) * hd]
        s = lax.dot_general(key, query, (((1,), (1,)), ((), ())), preferred_element_type=jnp.float32)
        t = s * scale + bias
        top = jnp.max(t, axis=0, keepdims=True)
        if first:
            m_new = top
        else:
            m_old = m_ref[row:row + 1, :]
            m_new = jnp.maximum(m_old, top)
        p = jnp.exp2(t - m_new)
        total = jnp.sum(p, axis=0, keepdims=True)
        part = jnp.dot(value_t, p.astype(jnp.bfloat16), preferred_element_type=jnp.float32)
        if first:
            l_ref[row:row + 1, :] = total
            acc_ref[row * hd:(row + 1) * hd, :] = part
        else:
            alpha = jnp.exp2(m_old - m_new)
            l_ref[row:row + 1, :] = l_ref[row:row + 1, :] * alpha + total
            acc_ref[row * hd:(row + 1) * hd, :] = acc_ref[row * hd:(row + 1) * hd, :] * alpha + part
        m_ref[row:row + 1, :] = m_new


def attend_chunk(dims, own, me, src, plan_ref, lengths_ref, *args):
    half = dims[0]
    order = [(0, 0), (1, 1), (0, 1), (1, 0)]
    lanes = lax.broadcasted_iota(jnp.int32, (1, half), 1)
    for q_blk, k_blk in order:
        q_base = plan_ref[me * 2 + q_blk] * half
        k_base = plan_ref[src * 2 + k_blk] * half
        if own and q_blk == k_blk:
            start = doc_start(lengths_ref, q_base + lanes)
            attend_pair(dims, True, True, q_blk, k_blk, start, k_base, *args)
        else:
            need = (k_base < q_base) & (scalar_start(lengths_ref, q_base) < k_base + half)

            @pl.when(need)
            def _(q_blk=q_blk, k_blk=k_blk, q_base=q_base, k_base=k_base):
                start = doc_start(lengths_ref, q_base + lanes)
                attend_pair(dims, False, False, q_blk, k_blk, start, k_base, *args)


def own_kernel(dims, plan_ref, lengths_ref, q_ref, k_ref, v_ref, m_ref, l_ref, acc_ref):
    me = lax.axis_index("ctx")
    attend_chunk(dims, True, me, me, plan_ref, lengths_ref, q_ref, k_ref, v_ref, m_ref, l_ref, acc_ref)


def copy_state(sources, targets):
    for source, target in zip(sources, targets):
        target[...] = source[...]


def chunk_kernel(dims, shift, plan_ref, lengths_ref, q_ref, k_ref, v_ref, m_in, l_in, acc_in, m_ref, l_ref, acc_ref):
    me = lax.axis_index("ctx")
    copy_state((m_in, l_in, acc_in), (m_ref, l_ref, acc_ref))
    attend_chunk(dims, False, me, me ^ shift, plan_ref, lengths_ref, q_ref, k_ref, v_ref, m_ref, l_ref, acc_ref)


def assemble_kernel(masks, *refs):
    part_refs, full_ref = refs[:-1], refs[-1]
    dp = lax.axis_index("dp")
    rows = part_refs[0].shape[1]
    for j, mask in enumerate(masks):
        for core in range(2):
            row = pl.multiple_of((dp ^ (mask ^ core)) * rows, rows)
            for i in range(full_ref.shape[0]):
                full_ref[i, pl.ds(row, rows), :] = part_refs[2 * j + core][i]


def final_kernel(dims, shift, groups, tile, *refs):
    half, hd, heads, _ = dims
    plan_ref, lengths_ref, q_ref, k_ref, v_ref, m_in, l_in, acc_in, w_ref = refs[:9]
    full_refs = refs[9:9 + len(groups)]
    out_ref, att, stage, m_ref, l_ref, acc_ref, o_sem = refs[9 + len(groups):]
    me = lax.axis_index("ctx")
    cols = w_ref.shape[1]
    copy_state((m_in, l_in, acc_in), (m_ref, l_ref, acc_ref))
    attend_chunk(dims, False, me, me ^ shift, plan_ref, lengths_ref, q_ref, k_ref, v_ref, m_ref, l_ref, acc_ref)
    for q_blk in range(2):
        for h in range(heads):
            row = q_blk * heads + h
            o = acc_ref[row * hd:(row + 1) * hd, :] / l_ref[row:row + 1, :]
            att[q_blk * half:(q_blk + 1) * half, h * hd:(h + 1) * hd] = o.T.astype(jnp.bfloat16)
    weights = [(0, w_ref)]
    for full_ref, shifts in zip(full_refs, groups):
        weights += [(s, full_ref.at[i]) for i, s in enumerate(shifts)]
    stores = []
    for slot, (s, weight) in enumerate(weights):
        base = (me ^ s) * cols
        for t in range(0, cols, tile):
            y = jnp.dot(att[...], weight[:, t:t + tile], preferred_element_type=jnp.float32)
            stage[slot, :, t:t + tile] = y.astype(jnp.bfloat16)
            store = pltpu.make_async_copy(
                stage.at[slot, :, pl.ds(t, tile)],
                out_ref.at[:, pl.ds(pl.multiple_of(base + t, tile), tile)],
                o_sem.at[slot, t // tile],
            )
            store.start()
            stores.append(store)
    for store in stores:
        store.wait()


def shards(dp_size, ctx, *args):
    return run(dp_size, ctx, *args)


def run(dp_size, ctx, queries, key_vectors, value_vectors, block_plan, doc_lengths, out_weight):
    rows, width = queries.shape
    hd = key_vectors.shape[1]
    heads = width // hd
    half = rows // 2
    depth, cols = out_weight.shape
    out_cols = cols * ctx
    piece_rows = depth // dp_size
    dims = (half, hd, heads, math.log2(math.e) / math.sqrt(hd))
    shifts = list(range(1, ctx))
    masks = list(range(0, dp_size, 2))
    groups = groups_of(ctx)

    def from_ctx(x, s):
        return lax.ppermute(x, "ctx", [(i ^ s, i) for i in range(ctx)])

    def from_dp(x, mask):
        return lax.ppermute(x, "dp", [(i ^ mask, i) for i in range(dp_size)])

    keys, values, w_z = {}, {}, {}
    for s in shifts:
        keys[s] = from_ctx(key_vectors, s)
        values[s] = from_ctx(value_vectors, s)
    piece = lax.dynamic_slice_in_dim(out_weight, lax.axis_index("dp") * piece_rows, piece_rows, 0)
    for s in shifts:
        w_z[s] = from_ctx(piece, s)

    smem = pl.BlockSpec(memory_space=pltpu.SMEM)
    vmem = pl.BlockSpec(memory_space=pltpu.VMEM)
    anyspace = pl.BlockSpec(memory_space=pl.ANY)
    state_shapes = (
        jax.ShapeDtypeStruct((2 * heads, half), jnp.float32),
        jax.ShapeDtypeStruct((2 * heads, half), jnp.float32),
        jax.ShapeDtypeStruct((2 * heads * hd, half), jnp.float32),
    )
    chunk_cost = pl.CostEstimate(
        flops=4 * heads * rows * rows * hd, bytes_accessed=3 * MIB, transcendentals=heads * rows * rows
    )
    state = pl.pallas_call(
        functools.partial(own_kernel, dims),
        out_shape=state_shapes,
        in_specs=[smem, smem, vmem, vmem, vmem],
        out_specs=(vmem,) * 3,
        compiler_params=pltpu.CompilerParams(vmem_limit_bytes=16 * MIB),
        cost_estimate=chunk_cost,
        name="attend_own",
    )(block_plan, doc_lengths, queries, key_vectors, value_vectors)
    for s in shifts[:-1]:
        state = pl.pallas_call(
            functools.partial(chunk_kernel, dims, s),
            out_shape=state_shapes,
            in_specs=[smem, smem] + [vmem] * 6,
            out_specs=(vmem,) * 3,
            compiler_params=pltpu.CompilerParams(vmem_limit_bytes=16 * MIB),
            cost_estimate=chunk_cost,
        )(block_plan, doc_lengths, queries, keys[s], values[s], *state)

    fulls = []
    for members in groups:
        mine = jnp.stack([w_z[s] for s in members])
        parts = []
        for mask in masks:
            part = mine
            if mask:
                part = from_dp(mine, mask)
            parts += [part, from_dp(part, 1)]
        fulls.append(
            pl.pallas_call(
                functools.partial(assemble_kernel, masks),
                out_shape=jax.ShapeDtypeStruct((len(members), depth, cols), jnp.bfloat16),
                in_specs=[vmem] * len(parts),
                out_specs=vmem,
                compiler_params=pltpu.CompilerParams(vmem_limit_bytes=16 * MIB),
                cost_estimate=pl.CostEstimate(flops=0, bytes_accessed=2 * MIB, transcendentals=0),
            )(*parts)
        )

    tile = min(cols, 512)
    last = shifts[-1]
    return pl.pallas_call(
        functools.partial(final_kernel, dims, last, groups, tile),
        out_shape=jax.ShapeDtypeStruct((rows, out_cols), jnp.bfloat16),
        in_specs=[smem, smem] + [vmem] * (7 + len(fulls)),
        out_specs=anyspace,
        scratch_shapes=[
            pltpu.VMEM((rows, width), jnp.bfloat16),
            pltpu.VMEM((ctx, rows, cols), jnp.bfloat16),
            pltpu.VMEM((2 * heads, half), jnp.float32),
            pltpu.VMEM((2 * heads, half), jnp.float32),
            pltpu.VMEM((2 * heads * hd, half), jnp.float32),
            pltpu.SemaphoreType.DMA((ctx, cols // tile)),
        ],
        compiler_params=pltpu.CompilerParams(vmem_limit_bytes=28 * MIB),
        cost_estimate=pl.CostEstimate(
            flops=2 * rows * depth * out_cols, bytes_accessed=8 * MIB, transcendentals=0
        ),
        name="project",
    )(block_plan, doc_lengths, queries, keys[last], values[last], *state, out_weight, *fulls)


def groups_of(ctx):
    shifts = list(range(1, ctx))
    return [shifts[:-1], shifts[-1:]] if ctx > 2 else [shifts]


def solution(mesh):
    placed = (
        P(("dp", "ctx"), None),
        P(("dp", "ctx"), None),
        P(("dp", "ctx"), None),
        P("dp"),
        P("dp"),
        P(None, "ctx"),
    )
    body = functools.partial(shards, mesh.shape["dp"], mesh.shape["ctx"])
    return jax.shard_map(body, mesh=mesh, in_specs=placed, out_specs=P(("dp", "ctx"), None), check_vma=False)
```

time: 63.7 us -> 66.6 us (1.046)
  the two profiles are of different devices: /device:TPU:0 before, /device:TPU:3 now
where the time goes in v2:
time: 66.6 us; the launch traced here: 66.4 us
  starting transfers between devices  27.3 us (41%)
  waiting for transfers between devices  18.6 us (28%)
  Pallas kernels  15 us (23%)
  local copies, waits for them, and re-layouts  5.1 us (8%)
    ppermute x14, starting transfers between devices, from_dp(): return lax.ppermute(x, 'dp', [(i ^ mask, i) for i in range(dp_size)])  14 us
    ppermute x9, starting transfers between devices, from_ctx(): return lax.ppermute(x, 'ctx', [(i ^ s, i) for i in range(ctx)])  13.3 us
    ppermute x9, waiting for transfers between devices, from_ctx(): return lax.ppermute(x, 'ctx', [(i ^ s, i) for i in range(ctx)])  13 us
    ppermute x14, waiting for transfers between devices, from_dp(): return lax.ppermute(x, 'dp', [(i ^ mask, i) for i in range(dp_size)])  5.62 us
    pallas_call x2, Pallas kernels, run(): pl.pallas_call(functools.partial(chunk_kernel, dims, s), out_shape=state_...  5.32 us
    pallas_call x1, Pallas kernels, run(): pl.pallas_call(functools.partial(final_kernel, dims, last, groups, tile),...  5.23 us
    pallas_call x1, Pallas kernels, run(): pl.pallas_call(functools.partial(own_kernel, dims), out_shape=state_shape...  4.27 us
    unnamed x18, local copies, waits for them, and re-layouts  4.18 us
  transfers between devices with their start and end apart: 23, of which 7 were waited for; matrix products, arithmetic and copies ran while one was open for 0% of the time, Pallas kernels for 15%

profile of v2, /device:TPU:3, one launch (start us, length us, event | category | flops | bytes accessed | tf_op | source)
XLA Modules:
  0.0 66.4 jit_solution(15734143720947778622)
XLA Ops:
  0.0 0.9 %constant_dynamic-slice_fusion = bf16[64,1024]{1,0:T(8,128)(2,1)S(1)} fusion(bf16[512,1024]{1,0:T(8,128)(2,1)} %refs_8_.1, s32[]{:T(128)S(6)} %select_n.3), kind=kLoop, calls=%fused_computation.1 | loop fusion | bytes 262148 | tf_op jit(solution)/shard_map/dynamic_slice | solution.py:174
  0.9 3.4 %collective-permute-start.15 = (bf16[64,1024]{1,0:T(8,128)(2,1)S(1)}, bf16[64,1024]{1,0:T(8,128)(2,1)S(1)}, u32[]{:S(2)}, u32[]{:S(2)}) collective-permute-start(bf16[64,1024]{1,0:T(8,128)(2,1)S(1)} %constant_dynamic-slice_fusion), channel_id=1, source_target_pairs={{3,0},{2,1},{1,2},{0,3},{7,4},{6,5},{5,6},{4,7},{11,8},{10,9},{9,1... | collective-permute-start | bytes 393224 | tf_op jit(solution)/shard_map/ppermute | solution.py:165
  4.3 0.0 collective-permute-start.7
  4.3 0.4 collective-permute-start.6
  4.7 2.0 %collective-permute-start.2 = (bf16[512,128]{1,0:T(8,128)(2,1)}, bf16[512,128]{1,0:T(8,128)(2,1)S(1)}, u32[]{:S(2)}, u32[]{:S(2)}) collective-permute-start(bf16[512,128]{1,0:T(8,128)(2,1)} %k_ref.1), channel_id=1, source_target_pairs={{2,0},{3,1},{0,2},{1,3},{6,4},{7,5},{4,6},{5,7},{10,8},{11,9},{8,1... | collective-permute-start | bytes 393224 | tf_op jit(solution)/shard_map/ppermute | solution.py:165
  6.7 1.5 %collective-permute-start.4 = (bf16[512,128]{1,0:T(8,128)(2,1)}, bf16[512,128]{1,0:T(8,128)(2,1)S(1)}, u32[]{:S(2)}, u32[]{:S(2)}) collective-permute-start(bf16[512,128]{1,0:T(8,128)(2,1)} %k_ref.1), channel_id=1, source_target_pairs={{1,0},{0,1},{3,2},{2,3},{5,4},{4,5},{7,6},{6,7},{9,8},{8,9},{11,10... | collective-permute-start | bytes 393224 | tf_op jit(solution)/shard_map/ppermute | solution.py:165
  8.1 2.7 %collective-permute-start.3 = (bf16[512,128]{1,0:T(8,128)(2,1)}, bf16[512,128]{1,0:T(8,128)(2,1)S(1)}, u32[]{:S(2)}, u32[]{:S(2)}) collective-permute-start(bf16[512,128]{1,0:T(8,128)(2,1)} %v_ref.1), channel_id=1, source_target_pairs={{2,0},{3,1},{0,2},{1,3},{6,4},{7,5},{4,6},{5,7},{10,8},{11,9},{8,1... | collective-permute-start | bytes 393224 | tf_op jit(solution)/shard_map/ppermute | solution.py:165
  10.9 6.8 %collective-permute-done.7 = bf16[64,1024]{1,0:T(8,128)(2,1)S(1)} collective-permute-done((bf16[64,1024]{1,0:T(8,128)(2,1)S(1)}, bf16[64,1024]{1,0:T(8,128)(2,1)S(1)}, u32[]{:S(2)}, u32[]{:S(2)}) %collective-permute-start.7) | collective-permute-done | bytes 131104 | tf_op jit(solution)/shard_map/ppermute | solution.py:165
  17.7 1.2 %collective-permute-start.21 = (bf16[1,64,1024]{2,1,0:T(8,128)(2,1)S(1)}, bf16[1,64,1024]{2,1,0:T(8,128)(2,1)S(1)}, u32[]{:S(2)}, u32[]{:S(2)}) collective-permute-start(bf16[1,64,1024]{2,1,0:T(8,128)(2,1)S(1)} %bitcast.3), channel_id=1, source_target_pairs={{24,0},{28,4},{16,8},{20,12},{8,16},{12,20},{0,24},{4,28},{25,1},{... | collective-permute-start | bytes 393224 | tf_op jit(solution)/shard_map/ppermute | solution.py:168
  18.9 0.0 collective-permute-done.6
  18.9 0.0 collective-permute-start.5
  19.0 4.4 %collective-permute-done.2.k_ref = bf16[512,128]{1,0:T(8,128)(2,1)S(1)} collective-permute-done((bf16[512,128]{1,0:T(8,128)(2,1)}, bf16[512,128]{1,0:T(8,128)(2,1)S(1)}, u32[]{:S(2)}, u32[]{:S(2)}) %collective-permute-start.2) | collective-permute-done | bytes 131104 | tf_op jit(solution)/shard_map/ppermute | solution.py:165
  23.4 1.2 %collective-permute-start.19 = (bf16[1,64,1024]{2,1,0:T(8,128)(2,1)S(1)}, bf16[1,64,1024]{2,1,0:T(8,128)(2,1)S(1)}, u32[]{:S(2)}, u32[]{:S(2)}) collective-permute-start(bf16[1,64,1024]{2,1,0:T(8,128)(2,1)S(1)} %bitcast.4), channel_id=1, source_target_pairs={{16,0},{20,4},{24,8},{28,12},{0,16},{4,20},{8,24},{12,28},{17,1},{... | collective-permute-start | bytes 393224 | tf_op jit(solution)/shard_map/ppermute | solution.py:168
  24.6 0.0 collective-permute-done.4.k_ref
  24.6 0.3 collective-permute-start.17
  24.8 1.4 %collective-permute-done.3.v_ref = bf16[512,128]{1,0:T(8,128)(2,1)S(1)} collective-permute-done((bf16[512,128]{1,0:T(8,128)(2,1)}, bf16[512,128]{1,0:T(8,128)(2,1)S(1)}, u32[]{:S(2)}, u32[]{:S(2)}) %collective-permute-start.3) | collective-permute-done | bytes 131104 | tf_op jit(solution)/shard_map/ppermute | solution.py:165
  26.3 1.6 %collective-permute-start.16 = (bf16[1,64,1024]{2,1,0:T(8,128)(2,1)S(1)}, bf16[1,64,1024]{2,1,0:T(8,128)(2,1)S(1)}, u32[]{:S(2)}, u32[]{:S(2)}) collective-permute-start(bf16[1,64,1024]{2,1,0:T(8,128)(2,1)S(1)} %bitcast.6), channel_id=1, source_target_pairs={{4,0},{0,4},{12,8},{8,12},{20,16},{16,20},{28,24},{24,28},{5,1},{1... | collective-permute-start | bytes 393224 | tf_op jit(solution)/shard_map/ppermute | solution.py:168
  27.9 0.1 collective-permute-start.22
  28.0 0.3 collective-permute-done.5.v_ref
  28.3 1.2 %collective-permute-start.13 = (bf16[2,64,1024]{2,1,0:T(8,128)(2,1)S(1)}, bf16[2,64,1024]{2,1,0:T(8,128)(2,1)S(1)}, u32[]{:S(2)}, u32[]{:S(2)}) collective-permute-start(bf16[2,64,1024]{2,1,0:T(8,128)(2,1)S(1)} %pad_maximum_fusion.refs_0_), channel_id=1, source_target_pairs={{24,0},{28,4},{16,8},{20,12},{8,16},{12,20},{0,24},{4,28},{25,1},{... | collective-permute-start | bytes 786440 | tf_op jit(solution)/shard_map/ppermute | solution.py:168
  29.4 1.3 %collective-permute-start.11 = (bf16[2,64,1024]{2,1,0:T(8,128)(2,1)S(1)}, bf16[2,64,1024]{2,1,0:T(8,128)(2,1)S(1)}, u32[]{:S(2)}, u32[]{:S(2)}) collective-permute-start(bf16[2,64,1024]{2,1,0:T(8,128)(2,1)S(1)} %pad_maximum_fusion.refs_0_), channel_id=1, source_target_pairs={{16,0},{20,4},{24,8},{28,12},{0,16},{4,20},{8,24},{12,28},{17,1},{... | collective-permute-start | bytes 786440 | tf_op jit(solution)/shard_map/ppermute | solution.py:168
  30.8 0.2 collective-permute-start.9
  30.9 2.1 %collective-permute-start.20 = (bf16[1,64,1024]{2,1,0:T(8,128)(2,1)S(1)}, bf16[1,64,1024]{2,1,0:T(8,128)(2,1)S(1)}, u32[]{:S(2)}, u32[]{:S(2)}) collective-permute-start(bf16[1,64,1024]{2,1,0:T(8,128)(2,1)S(1)} %collective-permute-done.19.refs_4_), channel_id=1, source_target_pairs={{4,0},{0,4},{12,8},{8,12},{20,16},{16,20},{28,24},{24,28},{5,1},{1... | collective-permute-start | bytes 393224 | tf_op jit(solution)/shard_map/ppermute | solution.py:168
  33.1 0.1 collective-permute-start.8
  33.1 0.9 %collective-permute-done.20.refs_5_ = bf16[1,64,1024]{2,1,0:T(8,128)(2,1)S(1)} collective-permute-done((bf16[1,64,1024]{2,1,0:T(8,128)(2,1)S(1)}, bf16[1,64,1024]{2,1,0:T(8,128)(2,1)S(1)}, u32[]{:S(2)}, u32[]{:S(2)}) %collective-permute-start.20) | collective-permute-done | bytes 131104 | tf_op jit(solution)/shard_map/ppermute | solution.py:168
  34.1 0.4 collective-permute-start.18
  34.4 1.4 %collective-permute-done.13.refs_6_ = bf16[2,64,1024]{2,1,0:T(8,128)(2,1)S(1)} collective-permute-done((bf16[2,64,1024]{2,1,0:T(8,128)(2,1)S(1)}, bf16[2,64,1024]{2,1,0:T(8,128)(2,1)S(1)}, u32[]{:S(2)}, u32[]{:S(2)}) %collective-permute-start.13) | collective-permute-done | bytes 262176 | tf_op jit(solution)/shard_map/ppermute | solution.py:168
  35.8 3.9 %collective-permute-start.14 = (bf16[2,64,1024]{2,1,0:T(8,128)(2,1)S(1)}, bf16[2,64,1024]{2,1,0:T(8,128)(2,1)S(1)}, u32[]{:S(2)}, u32[]{:S(2)}) collective-permute-start(bf16[2,64,1024]{2,1,0:T(8,128)(2,1)S(1)} %collective-permute-done.13.refs_6_), channel_id=1, source_target_pairs={{4,0},{0,4},{12,8},{8,12},{20,16},{16,20},{28,24},{24,28},{5,1},{1... | collective-permute-start | bytes 786440 | tf_op jit(solution)/shard_map/ppermute | solution.py:168
  39.7 3.3 %collective-permute-done.11.refs_4_ = bf16[2,64,1024]{2,1,0:T(8,128)(2,1)S(1)} collective-permute-done((bf16[2,64,1024]{2,1,0:T(8,128)(2,1)S(1)}, bf16[2,64,1024]{2,1,0:T(8,128)(2,1)S(1)}, u32[]{:S(2)}, u32[]{:S(2)}) %collective-permute-start.11) | collective-permute-done | bytes 262176 | tf_op jit(solution)/shard_map/ppermute | solution.py:168
  43.0 0.5 collective-permute-start.12
  43.5 0.0 collective-permute-start.10
  43.5 2.4 %collective-permute-start = (bf16[512,128]{1,0:T(8,128)(2,1)}, bf16[512,128]{1,0:T(8,128)(2,1)S(1)}, u32[]{:S(2)}, u32[]{:S(2)}) collective-permute-start(bf16[512,128]{1,0:T(8,128)(2,1)} %k_ref.1), channel_id=1, source_target_pairs={{3,0},{2,1},{1,2},{0,3},{7,4},{6,5},{5,6},{4,7},{11,8},{10,9},{9,1... | collective-permute-start | bytes 393224 | tf_op jit(solution)/shard_map/ppermute | solution.py:165
  46.0 0.9 %collective-permute-start.1 = (bf16[512,128]{1,0:T(8,128)(2,1)}, bf16[512,128]{1,0:T(8,128)(2,1)S(1)}, u32[]{:S(2)}, u32[]{:S(2)}) collective-permute-start(bf16[512,128]{1,0:T(8,128)(2,1)} %v_ref.1), channel_id=1, source_target_pairs={{3,0},{2,1},{1,2},{0,3},{7,4},{6,5},{5,6},{4,7},{11,8},{10,9},{9,1... | collective-permute-start | bytes 393224 | tf_op jit(solution)/shard_map/ppermute | solution.py:165
  46.9 1.0 %copy-done.1 = bf16[512,512]{1,0:T(8,128)(2,1)S(1)} copy-done((bf16[512,512]{1,0:T(8,128)(2,1)S(1)}, bf16[512,512]{1,0:T(8,128)(2,1)}, u32[]{:S(2)}) %copy-start.1) | copy-done | bytes 524312
  47.9 0.7 copy-done.3
  48.6 0.7 copy-done.5
  49.2 0.9 %copy-done.7 = bf16[512,128]{1,0:T(8,128)(2,1)S(1)} copy-done((bf16[512,128]{1,0:T(8,128)(2,1)S(1)}, bf16[512,128]{1,0:T(8,128)(2,1)}, u32[]{:S(2)}) %copy-start.7) | copy-done | bytes 131096
  50.1 0.9 %copy-done.8 = bf16[512,128]{1,0:T(8,128)(2,1)S(1)} copy-done((bf16[512,128]{1,0:T(8,128)(2,1)S(1)}, bf16[512,128]{1,0:T(8,128)(2,1)}, u32[]{:S(2)}) %copy-start.8) | copy-done | bytes 131096
  51.0 4.3 %attend_own.1 = (f32[8,256]{1,0:T(8,128)S(1)}, f32[8,256]{1,0:T(8,128)S(1)}, f32[1024,256]{1,0:T(8,128)S(1)}) custom-call(s32[8]{0:T(128)S(1)} %copy-done.3, s32[8]{0:T(128)S(1)} %copy-done.5, bf16[512,512]{1,0:T(8,128)(2,1)S(1)} %copy-done.1, bf16[512,128]{1,0:T(8,128)(2,1)S(1)} %copy-done.7, bf16[512,128]{1,0:T(8,128)(2,1)S(1)} %copy-done.8), custom_call_target="tpu_custom_call" | custom-call | flops 536870912 | bytes 3145728 | tf_op jit(solution)/shard_map/attend_own/pallas_call | solution.py:189
  55.3 1.9 %shard_map.64 = (f32[8,256]{1,0:T(8,128)S(1)}, f32[8,256]{1,0:T(8,128)S(1)}, f32[1024,256]{1,0:T(8,128)S(1)}) custom-call(s32[8]{0:T(128)S(1)} %copy-done.3, s32[8]{0:T(128)S(1)} %copy-done.5, bf16[512,512]{1,0:T(8,128)(2,1)S(1)} %copy-done.1, bf16[512,128]{1,0:T(8,128)(2,1)S(1)} %collective-permute-done.4.k_ref, ...), custom_call_target="tpu_custom_call" | custom-call | flops 536870912 | bytes 3145728 | tf_op jit(solution)/shard_map/pallas_call | solution.py:199
  57.2 0.0 copy-start
  57.3 0.0 copy-start.2
  57.3 0.0 copy-start.4
  57.3 0.0 copy-start.6
  57.3 3.4 %shard_map.65 = (f32[8,256]{1,0:T(8,128)S(1)}, f32[8,256]{1,0:T(8,128)S(1)}, f32[1024,256]{1,0:T(8,128)S(1)}) custom-call(s32[8]{0:T(128)S(1)} %copy-done.3, s32[8]{0:T(128)S(1)} %copy-done.5, bf16[512,512]{1,0:T(8,128)(2,1)S(1)} %copy-done.1, bf16[512,128]{1,0:T(8,128)(2,1)S(1)} %collective-permute-done.2.k_ref, ...), custom_call_target="tpu_custom_call" | custom-call | flops 536870912 | bytes 3145728 | tf_op jit(solution)/shard_map/pallas_call | solution.py:199
  60.7 0.1 shard_map.67.refs_10_
  60.8 0.2 shard_map.66.refs_9_
  61.0 5.2 %project.1 = bf16[512,4096]{1,0:T(8,128)(2,1)} custom-call(s32[8]{0:T(128)S(1)} %copy-done.4, s32[8]{0:T(128)S(1)} %copy-done.6, bf16[512,512]{1,0:T(8,128)(2,1)S(1)} %copy-done.2, bf16[512,128]{1,0:T(8,128)(2,1)S(1)} %collective-permute-done.refs_3_, bf16[512,128]{1,0:T(8,128)(2,1)S(1)} %collective-permute-done.1.refs_4_, ...), custom_call_target="tpu_custom_call" | custom-call | flops 2147483648 | bytes 8388608 | tf_op jit(solution)/shard_map/project/pallas_call | solution.py:230
  (24 shorter events, 0.1 us)
Async XLA Ops:
  0.9 7.2 %collective-permute-start.15 = (bf16[64,1024]{1,0:T(8,128)(2,1)S(1)}, bf16[64,1024]{1,0:T(8,128)(2,1)S(1)}, u32[]{:S(2)}, u32[]{:S(2)}) collective-permute-start(bf16[64,1024]{1,0:T(8,128)(2,1)S(1)} %constant_dynamic-slice_fusion), channel_id=1, source_target_pairs={{3,0},{2,1},{1,2},{0,3},{7,4},{6,5},{5,6},{4,7},{11,8},{10,9},{9,1... | collective-permute-start | bytes 393224 | tf_op jit(solution)/shard_map/ppermute | solution.py:165
  4.3 13.4 %collective-permute-start.7 = (bf16[64,1024]{1,0:T(8,128)(2,1)S(1)}, bf16[64,1024]{1,0:T(8,128)(2,1)S(1)}, u32[]{:S(2)}, u32[]{:S(2)}) collective-permute-start(bf16[64,1024]{1,0:T(8,128)(2,1)S(1)} %constant_dynamic-slice_fusion), channel_id=1, source_target_pairs={{2,0},{3,1},{0,2},{1,3},{6,4},{7,5},{4,6},{5,7},{10,8},{11,9},{8,1... | collective-permute-start | bytes 393224 | tf_op jit(solution)/shard_map/ppermute | solution.py:165
  4.3 14.6 %collective-permute-start.6 = (bf16[64,1024]{1,0:T(8,128)(2,1)S(1)}, bf16[64,1024]{1,0:T(8,128)(2,1)S(1)}, u32[]{:S(2)}, u32[]{:S(2)}) collective-permute-start(bf16[64,1024]{1,0:T(8,128)(2,1)S(1)} %constant_dynamic-slice_fusion), channel_id=1, source_target_pairs={{1,0},{0,1},{3,2},{2,3},{5,4},{4,5},{7,6},{6,7},{9,8},{8,9},{11,10... | collective-permute-start | bytes 393224 | tf_op jit(solution)/shard_map/ppermute | solution.py:165
  4.7 18.7 %collective-permute-start.2 = (bf16[512,128]{1,0:T(8,128)(2,1)}, bf16[512,128]{1,0:T(8,128)(2,1)S(1)}, u32[]{:S(2)}, u32[]{:S(2)}) collective-permute-start(bf16[512,128]{1,0:T(8,128)(2,1)} %k_ref.1), channel_id=1, source_target_pairs={{2,0},{3,1},{0,2},{1,3},{6,4},{7,5},{4,6},{5,7},{10,8},{11,9},{8,1... | collective-permute-start | bytes 393224 | tf_op jit(solution)/shard_map/ppermute | solution.py:165
  6.7 17.9 %collective-permute-start.4 = (bf16[512,128]{1,0:T(8,128)(2,1)}, bf16[512,128]{1,0:T(8,128)(2,1)S(1)}, u32[]{:S(2)}, u32[]{:S(2)}) collective-permute-start(bf16[512,128]{1,0:T(8,128)(2,1)} %k_ref.1), channel_id=1, source_target_pairs={{1,0},{0,1},{3,2},{2,3},{5,4},{4,5},{7,6},{6,7},{9,8},{8,9},{11,10... | collective-permute-start | bytes 393224 | tf_op jit(solution)/shard_map/ppermute | solution.py:165
  8.1 18.1 %collective-permute-start.3 = (bf16[512,128]{1,0:T(8,128)(2,1)}, bf16[512,128]{1,0:T(8,128)(2,1)S(1)}, u32[]{:S(2)}, u32[]{:S(2)}) collective-permute-start(bf16[512,128]{1,0:T(8,128)(2,1)} %v_ref.1), channel_id=1, source_target_pairs={{2,0},{3,1},{0,2},{1,3},{6,4},{7,5},{4,6},{5,7},{10,8},{11,9},{8,1... | collective-permute-start | bytes 393224 | tf_op jit(solution)/shard_map/ppermute | solution.py:165
  17.7 10.1 %collective-permute-start.21 = (bf16[1,64,1024]{2,1,0:T(8,128)(2,1)S(1)}, bf16[1,64,1024]{2,1,0:T(8,128)(2,1)S(1)}, u32[]{:S(2)}, u32[]{:S(2)}) collective-permute-start(bf16[1,64,1024]{2,1,0:T(8,128)(2,1)S(1)} %bitcast.3), channel_id=1, source_target_pairs={{24,0},{28,4},{16,8},{20,12},{8,16},{12,20},{0,24},{4,28},{25,1},{... | collective-permute-start | bytes 393224 | tf_op jit(solution)/shard_map/ppermute | solution.py:168
  18.9 9.3 %collective-permute-start.5 = (bf16[512,128]{1,0:T(8,128)(2,1)}, bf16[512,128]{1,0:T(8,128)(2,1)S(1)}, u32[]{:S(2)}, u32[]{:S(2)}) collective-permute-start(bf16[512,128]{1,0:T(8,128)(2,1)} %v_ref.1), channel_id=1, source_target_pairs={{1,0},{0,1},{3,2},{2,3},{5,4},{4,5},{7,6},{6,7},{9,8},{8,9},{11,10... | collective-permute-start | bytes 393224 | tf_op jit(solution)/shard_map/ppermute | solution.py:165
  23.4 6.1 %collective-permute-start.19 = (bf16[1,64,1024]{2,1,0:T(8,128)(2,1)S(1)}, bf16[1,64,1024]{2,1,0:T(8,128)(2,1)S(1)}, u32[]{:S(2)}, u32[]{:S(2)}) collective-permute-start(bf16[1,64,1024]{2,1,0:T(8,128)(2,1)S(1)} %bitcast.4), channel_id=1, source_target_pairs={{16,0},{20,4},{24,8},{28,12},{0,16},{4,20},{8,24},{12,28},{17,1},{... | collective-permute-start | bytes 393224 | tf_op jit(solution)/shard_map/ppermute | solution.py:168
  24.6 6.2 %collective-permute-start.17 = (bf16[1,64,1024]{2,1,0:T(8,128)(2,1)S(1)}, bf16[1,64,1024]{2,1,0:T(8,128)(2,1)S(1)}, u32[]{:S(2)}, u32[]{:S(2)}) collective-permute-start(bf16[1,64,1024]{2,1,0:T(8,128)(2,1)S(1)} %bitcast.5), channel_id=1, source_target_pairs={{8,0},{12,4},{0,8},{4,12},{24,16},{28,20},{16,24},{20,28},{9,1},{1... | collective-permute-start | bytes 393224 | tf_op jit(solution)/shard_map/ppermute | solution.py:168
  26.3 4.7 %collective-permute-start.16 = (bf16[1,64,1024]{2,1,0:T(8,128)(2,1)S(1)}, bf16[1,64,1024]{2,1,0:T(8,128)(2,1)S(1)}, u32[]{:S(2)}, u32[]{:S(2)}) collective-permute-start(bf16[1,64,1024]{2,1,0:T(8,128)(2,1)S(1)} %bitcast.6), channel_id=1, source_target_pairs={{4,0},{0,4},{12,8},{8,12},{20,16},{16,20},{28,24},{24,28},{5,1},{1... | collective-permute-start | bytes 393224 | tf_op jit(solution)/shard_map/ppermute | solution.py:168
  27.9 5.2 %collective-permute-start.22 = (bf16[1,64,1024]{2,1,0:T(8,128)(2,1)S(1)}, bf16[1,64,1024]{2,1,0:T(8,128)(2,1)S(1)}, u32[]{:S(2)}, u32[]{:S(2)}) collective-permute-start(bf16[1,64,1024]{2,1,0:T(8,128)(2,1)S(1)} %collective-permute-done.21.refs_6_), channel_id=1, source_target_pairs={{4,0},{0,4},{12,8},{8,12},{20,16},{16,20},{28,24},{24,28},{5,1},{1... | collective-permute-start | bytes 393224 | tf_op jit(solution)/shard_map/ppermute | solution.py:168
  28.3 7.5 %collective-permute-start.13 = (bf16[2,64,1024]{2,1,0:T(8,128)(2,1)S(1)}, bf16[2,64,1024]{2,1,0:T(8,128)(2,1)S(1)}, u32[]{:S(2)}, u32[]{:S(2)}) collective-permute-start(bf16[2,64,1024]{2,1,0:T(8,128)(2,1)S(1)} %pad_maximum_fusion.refs_0_), channel_id=1, source_target_pairs={{24,0},{28,4},{16,8},{20,12},{8,16},{12,20},{0,24},{4,28},{25,1},{... | collective-permute-start | bytes 786440 | tf_op jit(solution)/shard_map/ppermute | solution.py:168
  29.4 13.6 %collective-permute-start.11 = (bf16[2,64,1024]{2,1,0:T(8,128)(2,1)S(1)}, bf16[2,64,1024]{2,1,0:T(8,128)(2,1)S(1)}, u32[]{:S(2)}, u32[]{:S(2)}) collective-permute-start(bf16[2,64,1024]{2,1,0:T(8,128)(2,1)S(1)} %pad_maximum_fusion.refs_0_), channel_id=1, source_target_pairs={{16,0},{20,4},{24,8},{28,12},{0,16},{4,20},{8,24},{12,28},{17,1},{... | collective-permute-start | bytes 786440 | tf_op jit(solution)/shard_map/ppermute | solution.py:168
  30.8 12.8 %collective-permute-start.9 = (bf16[2,64,1024]{2,1,0:T(8,128)(2,1)S(1)}, bf16[2,64,1024]{2,1,0:T(8,128)(2,1)S(1)}, u32[]{:S(2)}, u32[]{:S(2)}) collective-permute-start(bf16[2,64,1024]{2,1,0:T(8,128)(2,1)S(1)} %pad_maximum_fusion.refs_0_), channel_id=1, source_target_pairs={{8,0},{12,4},{0,8},{4,12},{24,16},{28,20},{16,24},{20,28},{9,1},{1... | collective-permute-start | bytes 786440 | tf_op jit(solution)/shard_map/ppermute | solution.py:168
  30.9 3.1 %collective-permute-start.20 = (bf16[1,64,1024]{2,1,0:T(8,128)(2,1)S(1)}, bf16[1,64,1024]{2,1,0:T(8,128)(2,1)S(1)}, u32[]{:S(2)}, u32[]{:S(2)}) collective-permute-start(bf16[1,64,1024]{2,1,0:T(8,128)(2,1)S(1)} %collective-permute-done.19.refs_4_), channel_id=1, source_target_pairs={{4,0},{0,4},{12,8},{8,12},{20,16},{16,20},{28,24},{24,28},{5,1},{1... | collective-permute-start | bytes 393224 | tf_op jit(solution)/shard_map/ppermute | solution.py:168
  33.1 12.9 %collective-permute-start.8 = (bf16[2,64,1024]{2,1,0:T(8,128)(2,1)S(1)}, bf16[2,64,1024]{2,1,0:T(8,128)(2,1)S(1)}, u32[]{:S(2)}, u32[]{:S(2)}) collective-permute-start(bf16[2,64,1024]{2,1,0:T(8,128)(2,1)S(1)} %pad_maximum_fusion.refs_0_), channel_id=1, source_target_pairs={{4,0},{0,4},{12,8},{8,12},{20,16},{16,20},{28,24},{24,28},{5,1},{1... | collective-permute-start | bytes 786440 | tf_op jit(solution)/shard_map/ppermute | solution.py:168
  34.1 9.5 %collective-permute-start.18 = (bf16[1,64,1024]{2,1,0:T(8,128)(2,1)S(1)}, bf16[1,64,1024]{2,1,0:T(8,128)(2,1)S(1)}, u32[]{:S(2)}, u32[]{:S(2)}) collective-permute-start(bf16[1,64,1024]{2,1,0:T(8,128)(2,1)S(1)} %collective-permute-done.17.refs_2_), channel_id=1, source_target_pairs={{4,0},{0,4},{12,8},{8,12},{20,16},{16,20},{28,24},{24,28},{5,1},{1... | collective-permute-start | bytes 393224 | tf_op jit(solution)/shard_map/ppermute | solution.py:168
  35.8 25.0 %collective-permute-start.14 = (bf16[2,64,1024]{2,1,0:T(8,128)(2,1)S(1)}, bf16[2,64,1024]{2,1,0:T(8,128)(2,1)S(1)}, u32[]{:S(2)}, u32[]{:S(2)}) collective-permute-start(bf16[2,64,1024]{2,1,0:T(8,128)(2,1)S(1)} %collective-permute-done.13.refs_6_), channel_id=1, source_target_pairs={{4,0},{0,4},{12,8},{8,12},{20,16},{16,20},{28,24},{24,28},{5,1},{1... | collective-permute-start | bytes 786440 | tf_op jit(solution)/shard_map/ppermute | solution.py:168
  43.0 17.8 %collective-permute-start.12 = (bf16[2,64,1024]{2,1,0:T(8,128)(2,1)S(1)}, bf16[2,64,1024]{2,1,0:T(8,128)(2,1)S(1)}, u32[]{:S(2)}, u32[]{:S(2)}) collective-permute-start(bf16[2,64,1024]{2,1,0:T(8,128)(2,1)S(1)} %collective-permute-done.11.refs_4_), channel_id=1, source_target_pairs={{4,0},{0,4},{12,8},{8,12},{20,16},{16,20},{28,24},{24,28},{5,1},{1... | collective-permute-start | bytes 786440 | tf_op jit(solution)/shard_map/ppermute | solution.py:168
  43.5 17.3 %collective-permute-start.10 = (bf16[2,64,1024]{2,1,0:T(8,128)(2,1)S(1)}, bf16[2,64,1024]{2,1,0:T(8,128)(2,1)S(1)}, u32[]{:S(2)}, u32[]{:S(2)}) collective-permute-start(bf16[2,64,1024]{2,1,0:T(8,128)(2,1)S(1)} %collective-permute-done.9.refs_2_), channel_id=1, source_target_pairs={{4,0},{0,4},{12,8},{8,12},{20,16},{16,20},{28,24},{24,28},{5,1},{1... | collective-permute-start | bytes 786440 | tf_op jit(solution)/shard_map/ppermute | solution.py:168
  43.5 17.4 %collective-permute-start = (bf16[512,128]{1,0:T(8,128)(2,1)}, bf16[512,128]{1,0:T(8,128)(2,1)S(1)}, u32[]{:S(2)}, u32[]{:S(2)}) collective-permute-start(bf16[512,128]{1,0:T(8,128)(2,1)} %k_ref.1), channel_id=1, source_target_pairs={{3,0},{2,1},{1,2},{0,3},{7,4},{6,5},{5,6},{4,7},{11,8},{10,9},{9,1... | collective-permute-start | bytes 393224 | tf_op jit(solution)/shard_map/ppermute | solution.py:165
  46.0 15.0 %collective-permute-start.1 = (bf16[512,128]{1,0:T(8,128)(2,1)}, bf16[512,128]{1,0:T(8,128)(2,1)S(1)}, u32[]{:S(2)}, u32[]{:S(2)}) collective-permute-start(bf16[512,128]{1,0:T(8,128)(2,1)} %v_ref.1), channel_id=1, source_target_pairs={{3,0},{2,1},{1,2},{0,3},{7,4},{6,5},{5,6},{4,7},{11,8},{10,9},{9,1... | collective-permute-start | bytes 393224 | tf_op jit(solution)/shard_map/ppermute | solution.py:165
  46.9 1.0 %copy-start.1 = (bf16[512,512]{1,0:T(8,128)(2,1)S(1)}, bf16[512,512]{1,0:T(8,128)(2,1)}, u32[]{:S(2)}) copy-start(bf16[512,512]{1,0:T(8,128)(2,1)} %refs_2_.1) | copy-start | bytes 1572868
  47.9 0.7 copy-start.3
  48.6 0.7 copy-start.5
  49.2 0.9 %copy-start.7 = (bf16[512,128]{1,0:T(8,128)(2,1)S(1)}, bf16[512,128]{1,0:T(8,128)(2,1)}, u32[]{:S(2)}) copy-start(bf16[512,128]{1,0:T(8,128)(2,1)} %k_ref.1) | copy-start | bytes 393220
  50.1 0.9 %copy-start.8 = (bf16[512,128]{1,0:T(8,128)(2,1)S(1)}, bf16[512,128]{1,0:T(8,128)(2,1)}, u32[]{:S(2)}) copy-start(bf16[512,128]{1,0:T(8,128)(2,1)} %v_ref.1) | copy-start | bytes 393220
  57.2 3.7 %copy-start = (bf16[512,1024]{1,0:T(8,128)(2,1)S(1)}, bf16[512,1024]{1,0:T(8,128)(2,1)}, u32[]{:S(2)}) copy-start(bf16[512,1024]{1,0:T(8,128)(2,1)} %refs_8_.1) | copy-start | bytes 3145732
  57.3 3.7 %copy-start.2 = (bf16[512,512]{1,0:T(8,128)(2,1)S(1)}, bf16[512,512]{1,0:T(8,128)(2,1)}, u32[]{:S(2)}) copy-start(bf16[512,512]{1,0:T(8,128)(2,1)} %refs_2_.1) | copy-start | bytes 1572868
  57.3 3.7 %copy-start.4 = (s32[8]{0:T(128)S(1)}, s32[8]{0:T(128)}, u32[]{:S(2)}) copy-start(s32[8]{0:T(128)} %refs_0_.1) | copy-start | bytes 100
  57.3 3.7 %copy-start.6 = (s32[8]{0:T(128)S(1)}, s32[8]{0:T(128)}, u32[]{:S(2)}) copy-start(s32[8]{0:T(128)} %refs_1_.1) | copy-start | bytes 100

commit v3 on v2

v3 whole, which is shorter than its diff:
```python
import functools
import math

import jax
import jax.numpy as jnp
from jax import lax
from jax.experimental import pallas as pl
from jax.experimental.pallas import tpu as pltpu
from jax.sharding import PartitionSpec as P


NEG = -1e30
MIB = 1 << 20


def doc_start(lengths_ref, position):
    end = jnp.int32(0)
    start = jnp.zeros_like(position)
    for i in range(lengths_ref.shape[0]):
        end = end + lengths_ref[i]
        start = jnp.maximum(start, jnp.where(position >= end, end, 0))
    return start


def scalar_start(lengths_ref, position):
    end = jnp.int32(0)
    start = jnp.int32(0)
    for i in range(lengths_ref.shape[0]):
        end = end + lengths_ref[i]
        start = jnp.maximum(start, jnp.where(position >= end, end, 0))
    return start


def attend_pair(dims, first, diagonal, q_blk, k_blk, start, key_base, q_ref, kv_ref, m_ref, l_ref, acc_ref):
    half, hd, heads, scale = dims
    wide = heads * half
    key = kv_ref[0, k_blk * half:(k_blk + 1) * half, :]
    value_t = kv_ref[1, k_blk * half:(k_blk + 1) * half, :].astype(jnp.float32).T.astype(jnp.bfloat16)
    key_ids = lax.broadcasted_iota(jnp.int32, (half, half), 0)
    keep = key_ids >= start - key_base
    if diagonal:
        keep = keep & (key_ids <= lax.broadcasted_iota(jnp.int32, (half, half), 1))
    bias = jnp.where(keep, jnp.float32(0.0), jnp.float32(NEG))
    bias = jnp.concatenate([bias] * heads, axis=1)
    query = q_ref[q_blk * wide:(q_blk + 1) * wide, :]
    s = lax.dot_general(key, query, (((1,), (1,)), ((), ())), preferred_element_type=jnp.float32)
    t = s * scale + bias
    top = jnp.max(t, axis=0, keepdims=True)
    at = slice(q_blk, q_blk + 1)
    rows = slice(q_blk * hd, (q_blk + 1) * hd)
    if first:
        m_new = top
    else:
        m_old = m_ref[at, :]
        m_new = jnp.maximum(m_old, top)
    p = jnp.exp2(t - m_new)
    total = jnp.sum(p, axis=0, keepdims=True)
    part = jnp.dot(value_t, p.astype(jnp.bfloat16), preferred_element_type=jnp.float32)
    if first:
        l_ref[at, :] = total
        acc_ref[rows, :] = part
    else:
        alpha = jnp.exp2(m_old - m_new)
        l_ref[at, :] = l_ref[at, :] * alpha + total
        acc_ref[rows, :] = acc_ref[rows, :] * alpha + part
    m_ref[at, :] = m_new


def attend_chunk(dims, own, me, src, plan_ref, lengths_ref, *args):
    half = dims[0]
    order = [(0, 0), (1, 1), (0, 1), (1, 0)]
    lanes = lax.broadcasted_iota(jnp.int32, (1, half), 1)
    for q_blk, k_blk in order:
        q_base = plan_ref[me * 2 + q_blk] * half
        k_base = plan_ref[src * 2 + k_blk] * half
        if own and q_blk == k_blk:
            start = doc_start(lengths_ref, q_base + lanes)
            attend_pair(dims, True, True, q_blk, k_blk, start, k_base, *args)
        else:
            need = (k_base < q_base) & (scalar_start(lengths_ref, q_base) < k_base + half)

            @pl.when(need)
            def _(q_blk=q_blk, k_blk=k_blk, q_base=q_base, k_base=k_base):
                start = doc_start(lengths_ref, q_base + lanes)
                attend_pair(dims, False, False, q_blk, k_blk, start, k_base, *args)


def pack_kernel(k_ref, v_ref, w_ref, kv_ref, piece_ref, sem):
    rows = piece_ref.shape[0]
    base = pl.multiple_of(lax.axis_index("dp") * rows, rows)
    copies = [
        pltpu.make_async_copy(k_ref, kv_ref.at[0], sem.at[0]),
        pltpu.make_async_copy(v_ref, kv_ref.at[1], sem.at[1]),
        pltpu.make_async_copy(w_ref.at[pl.ds(base, rows), :], piece_ref, sem.at[2]),
    ]
    for copy in copies:
        copy.start()
    for copy in copies:
        copy.wait()


def own_kernel(dims, plan_hbm, lengths_hbm, q_hbm, kv_ref, q_ref, m_ref, l_ref, acc_ref, plan_ref, lengths_ref, sem):
    half, hd, heads, _ = dims
    me = lax.axis_index("ctx")
    copies = [
        pltpu.make_async_copy(plan_hbm, plan_ref, sem.at[0]),
        pltpu.make_async_copy(lengths_hbm, lengths_ref, sem.at[1]),
    ]
    for q_blk in range(2):
        for h in range(heads):
            row = (q_blk * heads + h) * half
            copies.append(
                pltpu.make_async_copy(
                    q_hbm.at[pl.ds(q_blk * half, half), pl.ds(h * hd, hd)],
                    q_ref.at[pl.ds(row, half), :],
                    sem.at[2 + q_blk * heads + h],
                )
            )
    for copy in copies:
        copy.start()
    for copy in copies:
        copy.wait()
    attend_chunk(dims, True, me, me, plan_ref, lengths_ref, q_ref, kv_ref, m_ref, l_ref, acc_ref)


def chunk_kernel(
    dims, shift, plan_hbm, lengths_hbm, q_ref, kv_ref, m_in, l_in, acc_in, m_ref, l_ref, acc_ref, plan_ref, lengths_ref, sem
):
    me = lax.axis_index("ctx")
    copies = [
        pltpu.make_async_copy(plan_hbm, plan_ref, sem.at[0]),
        pltpu.make_async_copy(lengths_hbm, lengths_ref, sem.at[1]),
    ]
    for copy in copies:
        copy.start()
    for source, target in ((m_in, m_ref), (l_in, l_ref), (acc_in, acc_ref)):
        target[...] = source[...]
    for copy in copies:
        copy.wait()
    attend_chunk(dims, False, me, me ^ shift, plan_ref, lengths_ref, q_ref, kv_ref, m_ref, l_ref, acc_ref)


def assemble_kernel(masks, *refs):
    part_refs, full_ref = refs[:-1], refs[-1]
    dp = lax.axis_index("dp")
    rows = part_refs[0].shape[1]
    for j, mask in enumerate(masks):
        for core in range(2):
            row = pl.multiple_of((dp ^ (mask ^ core)) * rows, rows)
            for i in range(full_ref.shape[0]):
                full_ref[i, pl.ds(row, rows), :] = part_refs[2 * j + core][i]


def final_kernel(dims, groups, tile, l_ref, acc_ref, w_ref, *refs):
    half, hd, heads, _ = dims
    full_refs = refs[:len(groups)]
    out_ref, att, stage, o_sem = refs[len(groups):]
    me = lax.axis_index("ctx")
    cols = w_ref.shape[1]
    for q_blk in range(2):
        o = acc_ref[q_blk * hd:(q_blk + 1) * hd, :] / l_ref[q_blk:q_blk + 1, :]
        for h in range(heads):
            block = o[:, h * half:(h + 1) * half].T
            att[q_blk * half:(q_blk + 1) * half, h * hd:(h + 1) * hd] = block.astype(jnp.bfloat16)
    weights = [(0, w_ref)]
    for full_ref, shifts in zip(full_refs, groups):
        weights += [(s, full_ref.at[i]) for i, s in enumerate(shifts)]
    stores = []
    for slot, (s, weight) in enumerate(weights):
        base = (me ^ s) * cols
        for t in range(0, cols, tile):
            y = jnp.dot(att[...], weight[:, t:t + tile], preferred_element_type=jnp.float32)
            stage[slot, :, t:t + tile] = y.astype(jnp.bfloat16)
            store = pltpu.make_async_copy(
                stage.at[slot, :, pl.ds(t, tile)],
                out_ref.at[:, pl.ds(pl.multiple_of(base + t, tile), tile)],
                o_sem.at[slot, t // tile],
            )
            store.start()
            stores.append(store)
    for store in stores:
        store.wait()


def shards(dp_size, ctx, *args):
    return run(dp_size, ctx, *args)


def run(dp_size, ctx, queries, key_vectors, value_vectors, block_plan, doc_lengths, out_weight):
    rows, width = queries.shape
    hd = key_vectors.shape[1]
    heads = width // hd
    half = rows // 2
    depth, cols = out_weight.shape
    out_cols = cols * ctx
    piece_rows = depth // dp_size
    dims = (half, hd, heads, math.log2(math.e) / math.sqrt(hd))
    shifts = list(range(1, ctx))
    masks = list(range(0, dp_size, 2))
    groups = groups_of(ctx)
    vmem = pl.BlockSpec(memory_space=pltpu.VMEM)
    hbm = pl.BlockSpec(memory_space=pltpu.HBM)

    def in_hbm(x):
        return pltpu.with_memory_space_constraint(x, pltpu.HBM)

    def params(mib):
        return pltpu.CompilerParams(vmem_limit_bytes=mib * MIB)

    def from_ctx(x, s):
        return lax.ppermute(x, "ctx", [(i ^ s, i) for i in range(ctx)])

    def from_dp(x, mask):
        return lax.ppermute(x, "dp", [(i ^ mask, i) for i in range(dp_size)])

    kv_own, piece = pl.pallas_call(
        pack_kernel,
        out_shape=(
            jax.ShapeDtypeStruct((2, rows, hd), jnp.bfloat16),
            jax.ShapeDtypeStruct((piece_rows, cols), jnp.bfloat16),
        ),
        in_specs=[hbm] * 3,
        out_specs=(vmem, vmem),
        scratch_shapes=[pltpu.SemaphoreType.DMA((3,))],
        compiler_params=params(4),
        name="pack",
    )(in_hbm(key_vectors), in_hbm(value_vectors), in_hbm(out_weight))
    kv, w_z = {}, {}
    for s in shifts:
        kv[s] = from_ctx(kv_own, s)
    for s in shifts:
        w_z[s] = from_ctx(piece, s)

    state_shapes = (
        jax.ShapeDtypeStruct((2, heads * half), jnp.float32),
        jax.ShapeDtypeStruct((2, heads * half), jnp.float32),
        jax.ShapeDtypeStruct((2 * hd, heads * half), jnp.float32),
    )
    chunk_cost = pl.CostEstimate(
        flops=4 * heads * rows * rows * hd, bytes_accessed=3 * MIB, transcendentals=heads * rows * rows
    )
    stacked, *state = pl.pallas_call(
        functools.partial(own_kernel, dims),
        out_shape=(jax.ShapeDtypeStruct((rows * heads, hd), jnp.bfloat16),) + state_shapes,
        in_specs=[hbm, hbm, hbm, vmem],
        out_specs=(vmem,) * 4,
        scratch_shapes=[
            pltpu.SMEM(block_plan.shape, jnp.int32),
            pltpu.SMEM(doc_lengths.shape, jnp.int32),
            pltpu.SemaphoreType.DMA((2 + 2 * heads,)),
        ],
        compiler_params=params(16),
        cost_estimate=chunk_cost,
        name="attend_own",
    )(in_hbm(block_plan), in_hbm(doc_lengths), in_hbm(queries), kv_own)
    for s in shifts:
        state = pl.pallas_call(
            functools.partial(chunk_kernel, dims, s),
            out_shape=state_shapes,
            in_specs=[hbm, hbm] + [vmem] * 5,
            out_specs=(vmem,) * 3,
            scratch_shapes=[
                pltpu.SMEM(block_plan.shape, jnp.int32),
                pltpu.SMEM(doc_lengths.shape, jnp.int32),
                pltpu.SemaphoreType.DMA((2,)),
            ],
            compiler_params=params(16),
            cost_estimate=chunk_cost,
        )(in_hbm(block_plan), in_hbm(doc_lengths), stacked, kv[s], *state)

    fulls = []
    for members in groups:
        mine = jnp.stack([w_z[s] for s in members])
        parts = []
        for mask in masks:
            part = mine
            if mask:
                part = from_dp(mine, mask)
            parts += [part, from_dp(part, 1)]
        fulls.append(
            pl.pallas_call(
                functools.partial(assemble_kernel, masks),
                out_shape=jax.ShapeDtypeStruct((len(members), depth, cols), jnp.bfloat16),
                in_specs=[vmem] * len(parts),
                out_specs=vmem,
                compiler_params=params(16),
                cost_estimate=pl.CostEstimate(flops=0, bytes_accessed=2 * MIB, transcendentals=0),
            )(*parts)
        )

    tile = min(cols, 512)
    return pl.pallas_call(
        functools.partial(final_kernel, dims, groups, tile),
        out_shape=jax.ShapeDtypeStruct((rows, out_cols), jnp.bfloat16),
        in_specs=[vmem] * (3 + len(fulls)),
        out_specs=hbm,
        scratch_shapes=[
            pltpu.VMEM((rows, width), jnp.bfloat16),
            pltpu.VMEM((ctx, rows, cols), jnp.bfloat16),
            pltpu.SemaphoreType.DMA((ctx, cols // tile)),
        ],
        compiler_params=params(24),
        cost_estimate=pl.CostEstimate(
            flops=2 * rows * depth * out_cols, bytes_accessed=8 * MIB, transcendentals=0
        ),
        name="project",
    )(state[1], state[2], out_weight, *fulls)


def groups_of(ctx):
    return [list(range(1, ctx))]


def solution(mesh):
    placed = (
        P(("dp", "ctx"), None),
        P(("dp", "ctx"), None),
        P(("dp", "ctx"), None),
        P("dp"),
        P("dp"),
        P(None, "ctx"),
    )
    body = functools.partial(shards, mesh.shape["dp"], mesh.shape["ctx"])
    return jax.shard_map(body, mesh=mesh, in_specs=placed, out_specs=P(("dp", "ctx"), None), check_vma=False)
```

time: 66.6 us -> 54.1 us (0.81)
  the two profiles are of different devices: /device:TPU:3 before, /device:TPU:18 now
where the time goes in v3:
time: 54.1 us; the launch traced here: 53.9 us
  waiting for transfers between devices  26.5 us (49%)
  Pallas kernels  13.9 us (26%)
  starting transfers between devices  13.2 us (24%)
    ppermute x6, waiting for transfers between devices, from_ctx(): return lax.ppermute(x, 'ctx', [(i ^ s, i) for i in range(ctx)])  22.9 us
    ppermute x6, starting transfers between devices, from_ctx(): return lax.ppermute(x, 'ctx', [(i ^ s, i) for i in range(ctx)])  8.75 us
    pallas_call x3, Pallas kernels, run(): pl.pallas_call(functools.partial(chunk_kernel, dims, s), out_shape=state_...  6.33 us
    ppermute x7, starting transfers between devices, from_dp(): return lax.ppermute(x, 'dp', [(i ^ mask, i) for i in range(dp_size)])  4.49 us
    ppermute x7, waiting for transfers between devices, from_dp(): return lax.ppermute(x, 'dp', [(i ^ mask, i) for i in range(dp_size)])  3.68 us
    pallas_call x1, Pallas kernels, run(): pl.pallas_call(functools.partial(final_kernel, dims, groups, tile), out_s...  3.32 us
    pallas_call x1, Pallas kernels, run(): pl.pallas_call(functools.partial(own_kernel, dims), out_shape=(jax.ShapeD...  2.98 us
  transfers between devices with their start and end apart: 13, of which 5 were waited for; matrix products, arithmetic and copies ran while one was open for 0% of the time, Pallas kernels for 17%

profile of v3, /device:TPU:18, one launch (start us, length us, event | category | flops | bytes accessed | tf_op | source)
XLA Modules:
  0.0 53.9 jit_solution(8504521558250112462)
XLA Ops:
  0.0 1.1 %pack.1 = (bf16[2,512,128]{2,1,0:T(8,128)(2,1)S(1)}, bf16[64,1024]{1,0:T(8,128)(2,1)S(1)}) custom-call(bf16[512,128]{1,0:T(8,128)(2,1)} %k_ref.1, bf16[512,128]{1,0:T(8,128)(2,1)} %v_ref.1, bf16[512,1024]{1,0:T(8,128)(2,1)} %w_ref.3), custom_call_target="tpu_custom_call" | custom-call | tf_op jit(solution)/shard_map/pack/pallas_call | solution.py:216
  1.1 0.5 collective-permute-start.5
  1.6 3.5 %collective-permute-start.4 = (bf16[64,1024]{1,0:T(8,128)(2,1)S(1)}, bf16[64,1024]{1,0:T(8,128)(2,1)S(1)}, u32[]{:S(2)}, u32[]{:S(2)}) collective-permute-start(bf16[64,1024]{1,0:T(8,128)(2,1)S(1)} %get-tuple-element.32), channel_id=1, source_target_pairs={{2,0},{3,1},{0,2},{1,3},{6,4},{7,5},{4,6},{5,7},{10,8},{11,9},{8,1... | collective-permute-start | bytes 393224 | tf_op jit(solution)/shard_map/ppermute | solution.py:211
  5.1 0.0 collective-permute-start.3
  5.1 8.0 %collective-permute-done.5 = bf16[64,1024]{1,0:T(8,128)(2,1)S(1)} collective-permute-done((bf16[64,1024]{1,0:T(8,128)(2,1)S(1)}, bf16[64,1024]{1,0:T(8,128)(2,1)S(1)}, u32[]{:S(2)}, u32[]{:S(2)}) %collective-permute-start.5) | collective-permute-done | bytes 131104 | tf_op jit(solution)/shard_map/ppermute | solution.py:211
  13.1 0.0 collective-permute-done.4
  13.1 0.0 collective-permute-done.3
  13.2 1.6 %collective-permute-start.11 = (bf16[3,64,1024]{2,1,0:T(8,128)(2,1)S(1)}, bf16[3,64,1024]{2,1,0:T(8,128)(2,1)S(1)}, u32[]{:S(2)}, u32[]{:S(2)}) collective-permute-start(bf16[3,64,1024]{2,1,0:T(8,128)(2,1)S(1)} %pad_maximum_fusion.refs_0_), channel_id=1, source_target_pairs={{24,0},{28,4},{16,8},{20,12},{8,16},{12,20},{0,24},{4,28},{25,1},{... | collective-permute-start | bytes 1179656 | tf_op jit(solution)/shard_map/ppermute | solution.py:214
  14.7 0.5 collective-permute-start.9
  15.2 1.5 %collective-permute-start.7 = (bf16[3,64,1024]{2,1,0:T(8,128)(2,1)S(1)}, bf16[3,64,1024]{2,1,0:T(8,128)(2,1)S(1)}, u32[]{:S(2)}, u32[]{:S(2)}) collective-permute-start(bf16[3,64,1024]{2,1,0:T(8,128)(2,1)S(1)} %pad_maximum_fusion.refs_0_), channel_id=1, source_target_pairs={{8,0},{12,4},{0,8},{4,12},{24,16},{28,20},{16,24},{20,28},{9,1},{1... | collective-permute-start | bytes 1179656 | tf_op jit(solution)/shard_map/ppermute | solution.py:214
  16.7 3.1 %collective-permute-start.2 = (bf16[2,512,128]{2,1,0:T(8,128)(2,1)S(1)}, bf16[2,512,128]{2,1,0:T(8,128)(2,1)S(1)}, u32[]{:S(2)}, u32[]{:S(2)}) collective-permute-start(bf16[2,512,128]{2,1,0:T(8,128)(2,1)S(1)} %get-tuple-element.19.kv_ref), channel_id=1, source_target_pairs={{1,0},{0,1},{3,2},{2,3},{5,4},{4,5},{7,6},{6,7},{9,8},{8,9},{11,10... | collective-permute-start | bytes 786440 | tf_op jit(solution)/shard_map/ppermute | solution.py:211
  19.9 0.0 collective-permute-start.1
  19.9 8.4 %collective-permute-done.2.kv_ref = bf16[2,512,128]{2,1,0:T(8,128)(2,1)S(1)} collective-permute-done((bf16[2,512,128]{2,1,0:T(8,128)(2,1)S(1)}, bf16[2,512,128]{2,1,0:T(8,128)(2,1)S(1)}, u32[]{:S(2)}, u32[]{:S(2)}) %collective-permute-start.2) | collective-permute-done | bytes 262176 | tf_op jit(solution)/shard_map/ppermute | solution.py:211
  28.3 0.0 collective-permute-start.6
  28.3 0.0 collective-permute-done.11.refs_6_
  28.3 0.5 collective-permute-start.12
  28.8 3.6 %collective-permute-done.9.refs_4_ = bf16[3,64,1024]{2,1,0:T(8,128)(2,1)S(1)} collective-permute-done((bf16[3,64,1024]{2,1,0:T(8,128)(2,1)S(1)}, bf16[3,64,1024]{2,1,0:T(8,128)(2,1)S(1)}, u32[]{:S(2)}, u32[]{:S(2)}) %collective-permute-start.9) | collective-permute-done | bytes 393248 | tf_op jit(solution)/shard_map/ppermute | solution.py:214
  32.4 0.0 collective-permute-start.10
  32.4 0.1 collective-permute-done.7.refs_2_
  32.5 0.4 collective-permute-start.8
  32.9 0.0 collective-permute-done.1.kv_ref
  32.9 1.6 %collective-permute-start = (bf16[2,512,128]{2,1,0:T(8,128)(2,1)S(1)}, bf16[2,512,128]{2,1,0:T(8,128)(2,1)S(1)}, u32[]{:S(2)}, u32[]{:S(2)}) collective-permute-start(bf16[2,512,128]{2,1,0:T(8,128)(2,1)S(1)} %get-tuple-element.19.kv_ref), channel_id=1, source_target_pairs={{3,0},{2,1},{1,2},{0,3},{7,4},{6,5},{5,6},{4,7},{11,8},{10,9},{9,1... | collective-permute-start | bytes 786440 | tf_op jit(solution)/shard_map/ppermute | solution.py:211
  34.5 3.0 %attend_own.1 = (bf16[2048,128]{1,0:T(8,128)(2,1)S(1)}, f32[2,1024]{1,0:T(2,128)S(1)}, f32[2,1024]{1,0:T(2,128)S(1)}, f32[256,1024]{1,0:T(8,128)S(1)}) custom-call(s32[8]{0:T(128)} %plan_hbm.7, s32[8]{0:T(128)} %lengths_hbm.7, bf16[512,512]{1,0:T(8,128)(2,1)} %q_hbm.1, bf16[2,512,128]{2,1,0:T(8,128)(2,1)S(1)} %get-tuple-element.19.kv_ref), custom_call_target="tpu_custom_call" | custom-call | flops 536870912 | bytes 3145728 | tf_op jit(solution)/shard_map/attend_own/pallas_call | solution.py:242
  37.5 2.1 %shard_map.64 = (f32[2,1024]{1,0:T(2,128)S(1)}, f32[2,1024]{1,0:T(2,128)S(1)}, f32[256,1024]{1,0:T(8,128)S(1)}) custom-call(s32[8]{0:T(128)} %plan_hbm.7, s32[8]{0:T(128)} %lengths_hbm.7, bf16[2048,128]{1,0:T(8,128)(2,1)S(1)} %get-tuple-element.20.q_ref, bf16[2,512,128]{2,1,0:T(8,128)(2,1)S(1)} %collective-permute-done.2.kv_ref, ...), custom_call_target="tpu_custom_call" | custom-call | flops 536870912 | bytes 3145728 | tf_op jit(solution)/shard_map/pallas_call | solution.py:257
  39.6 0.8 %shard_map.65 = (f32[2,1024]{1,0:T(2,128)S(1)}, f32[2,1024]{1,0:T(2,128)S(1)}, f32[256,1024]{1,0:T(8,128)S(1)}) custom-call(s32[8]{0:T(128)} %plan_hbm.7, s32[8]{0:T(128)} %lengths_hbm.7, bf16[2048,128]{1,0:T(8,128)(2,1)S(1)} %get-tuple-element.20.q_ref, bf16[2,512,128]{2,1,0:T(8,128)(2,1)S(1)} %collective-permute-done.1.kv_ref, ...), custom_call_target="tpu_custom_call" | custom-call | flops 536870912 | bytes 3145728 | tf_op jit(solution)/shard_map/pallas_call | solution.py:257
  40.4 0.0 copy-start
  40.5 6.4 %collective-permute-done.kv_ref = bf16[2,512,128]{2,1,0:T(8,128)(2,1)S(1)} collective-permute-done((bf16[2,512,128]{2,1,0:T(8,128)(2,1)S(1)}, bf16[2,512,128]{2,1,0:T(8,128)(2,1)S(1)}, u32[]{:S(2)}, u32[]{:S(2)}) %collective-permute-start) | collective-permute-done | bytes 262176 | tf_op jit(solution)/shard_map/ppermute | solution.py:211
  46.8 3.4 %shard_map.66 = (f32[2,1024]{1,0:T(2,128)}, f32[2,1024]{1,0:T(2,128)S(1)}, f32[256,1024]{1,0:T(8,128)S(1)}) custom-call(s32[8]{0:T(128)} %plan_hbm.7, s32[8]{0:T(128)} %lengths_hbm.7, bf16[2048,128]{1,0:T(8,128)(2,1)S(1)} %get-tuple-element.20.q_ref, bf16[2,512,128]{2,1,0:T(8,128)(2,1)S(1)} %collective-permute-done.kv_ref, ...), custom_call_target="tpu_custom_call" | custom-call | flops 536870912 | bytes 3145728 | tf_op jit(solution)/shard_map/pallas_call | solution.py:257
  50.3 0.0 collective-permute-done.6.refs_1_
  50.3 0.0 collective-permute-done.12.refs_7_
  50.3 0.0 collective-permute-done.10.refs_5_
  50.3 0.0 collective-permute-done.8.refs_3_
  50.3 0.2 shard_map.67.refs_0_
  50.5 0.0 copy-done
  50.5 3.3 %project.1 = bf16[512,4096]{1,0:T(8,128)(2,1)} custom-call(f32[2,1024]{1,0:T(2,128)S(1)} %get-tuple-element.30.l_ref, f32[256,1024]{1,0:T(8,128)S(1)} %get-tuple-element.31.acc_ref, bf16[512,1024]{1,0:T(8,128)(2,1)S(1)} %copy-done, bf16[3,512,1024]{2,1,0:T(8,128)(2,1)S(1)} %shard_map.67.refs_0_), custom_call_target="tpu_custom_call" | custom-call | flops 2147483648 | bytes 8388608 | tf_op jit(solution)/shard_map/project/pallas_call | solution.py:292
  (1 shorter events, 0.0 us)
Async XLA Ops:
  1.1 12.1 %collective-permute-start.5 = (bf16[64,1024]{1,0:T(8,128)(2,1)S(1)}, bf16[64,1024]{1,0:T(8,128)(2,1)S(1)}, u32[]{:S(2)}, u32[]{:S(2)}) collective-permute-start(bf16[64,1024]{1,0:T(8,128)(2,1)S(1)} %get-tuple-element.32), channel_id=1, source_target_pairs={{3,0},{2,1},{1,2},{0,3},{7,4},{6,5},{5,6},{4,7},{11,8},{10,9},{9,1... | collective-permute-start | bytes 393224 | tf_op jit(solution)/shard_map/ppermute | solution.py:211
  1.6 11.5 %collective-permute-start.4 = (bf16[64,1024]{1,0:T(8,128)(2,1)S(1)}, bf16[64,1024]{1,0:T(8,128)(2,1)S(1)}, u32[]{:S(2)}, u32[]{:S(2)}) collective-permute-start(bf16[64,1024]{1,0:T(8,128)(2,1)S(1)} %get-tuple-element.32), channel_id=1, source_target_pairs={{2,0},{3,1},{0,2},{1,3},{6,4},{7,5},{4,6},{5,7},{10,8},{11,9},{8,1... | collective-permute-start | bytes 393224 | tf_op jit(solution)/shard_map/ppermute | solution.py:211
  5.1 8.1 %collective-permute-start.3 = (bf16[64,1024]{1,0:T(8,128)(2,1)S(1)}, bf16[64,1024]{1,0:T(8,128)(2,1)S(1)}, u32[]{:S(2)}, u32[]{:S(2)}) collective-permute-start(bf16[64,1024]{1,0:T(8,128)(2,1)S(1)} %get-tuple-element.32), channel_id=1, source_target_pairs={{1,0},{0,1},{3,2},{2,3},{5,4},{4,5},{7,6},{6,7},{9,8},{8,9},{11,10... | collective-permute-start | bytes 393224 | tf_op jit(solution)/shard_map/ppermute | solution.py:211
  13.2 15.1 %collective-permute-start.11 = (bf16[3,64,1024]{2,1,0:T(8,128)(2,1)S(1)}, bf16[3,64,1024]{2,1,0:T(8,128)(2,1)S(1)}, u32[]{:S(2)}, u32[]{:S(2)}) collective-permute-start(bf16[3,64,1024]{2,1,0:T(8,128)(2,1)S(1)} %pad_maximum_fusion.refs_0_), channel_id=1, source_target_pairs={{24,0},{28,4},{16,8},{20,12},{8,16},{12,20},{0,24},{4,28},{25,1},{... | collective-permute-start | bytes 1179656 | tf_op jit(solution)/shard_map/ppermute | solution.py:214
  14.7 17.7 %collective-permute-start.9 = (bf16[3,64,1024]{2,1,0:T(8,128)(2,1)S(1)}, bf16[3,64,1024]{2,1,0:T(8,128)(2,1)S(1)}, u32[]{:S(2)}, u32[]{:S(2)}) collective-permute-start(bf16[3,64,1024]{2,1,0:T(8,128)(2,1)S(1)} %pad_maximum_fusion.refs_0_), channel_id=1, source_target_pairs={{16,0},{20,4},{24,8},{28,12},{0,16},{4,20},{8,24},{12,28},{17,1},{... | collective-permute-start | bytes 1179656 | tf_op jit(solution)/shard_map/ppermute | solution.py:214
  15.2 17.3 %collective-permute-start.7 = (bf16[3,64,1024]{2,1,0:T(8,128)(2,1)S(1)}, bf16[3,64,1024]{2,1,0:T(8,128)(2,1)S(1)}, u32[]{:S(2)}, u32[]{:S(2)}) collective-permute-start(bf16[3,64,1024]{2,1,0:T(8,128)(2,1)S(1)} %pad_maximum_fusion.refs_0_), channel_id=1, source_target_pairs={{8,0},{12,4},{0,8},{4,12},{24,16},{28,20},{16,24},{20,28},{9,1},{1... | collective-permute-start | bytes 1179656 | tf_op jit(solution)/shard_map/ppermute | solution.py:214
  16.7 11.6 %collective-permute-start.2 = (bf16[2,512,128]{2,1,0:T(8,128)(2,1)S(1)}, bf16[2,512,128]{2,1,0:T(8,128)(2,1)S(1)}, u32[]{:S(2)}, u32[]{:S(2)}) collective-permute-start(bf16[2,512,128]{2,1,0:T(8,128)(2,1)S(1)} %get-tuple-element.19.kv_ref), channel_id=1, source_target_pairs={{1,0},{0,1},{3,2},{2,3},{5,4},{4,5},{7,6},{6,7},{9,8},{8,9},{11,10... | collective-permute-start | bytes 786440 | tf_op jit(solution)/shard_map/ppermute | solution.py:211
  19.9 13.0 %collective-permute-start.1 = (bf16[2,512,128]{2,1,0:T(8,128)(2,1)S(1)}, bf16[2,512,128]{2,1,0:T(8,128)(2,1)S(1)}, u32[]{:S(2)}, u32[]{:S(2)}) collective-permute-start(bf16[2,512,128]{2,1,0:T(8,128)(2,1)S(1)} %get-tuple-element.19.kv_ref), channel_id=1, source_target_pairs={{2,0},{3,1},{0,2},{1,3},{6,4},{7,5},{4,6},{5,7},{10,8},{11,9},{8,1... | collective-permute-start | bytes 786440 | tf_op jit(solution)/shard_map/ppermute | solution.py:211
  28.3 22.0 %collective-permute-start.6 = (bf16[3,64,1024]{2,1,0:T(8,128)(2,1)S(1)}, bf16[3,64,1024]{2,1,0:T(8,128)(2,1)S(1)}, u32[]{:S(2)}, u32[]{:S(2)}) collective-permute-start(bf16[3,64,1024]{2,1,0:T(8,128)(2,1)S(1)} %pad_maximum_fusion.refs_0_), channel_id=1, source_target_pairs={{4,0},{0,4},{12,8},{8,12},{20,16},{16,20},{28,24},{24,28},{5,1},{1... | collective-permute-start | bytes 1179656 | tf_op jit(solution)/shard_map/ppermute | solution.py:214
  28.3 22.0 %collective-permute-start.12 = (bf16[3,64,1024]{2,1,0:T(8,128)(2,1)S(1)}, bf16[3,64,1024]{2,1,0:T(8,128)(2,1)S(1)}, u32[]{:S(2)}, u32[]{:S(2)}) collective-permute-start(bf16[3,64,1024]{2,1,0:T(8,128)(2,1)S(1)} %collective-permute-done.11.refs_6_), channel_id=1, source_target_pairs={{4,0},{0,4},{12,8},{8,12},{20,16},{16,20},{28,24},{24,28},{5,1},{1... | collective-permute-start | bytes 1179656 | tf_op jit(solution)/shard_map/ppermute | solution.py:214
  32.4 17.9 %collective-permute-start.10 = (bf16[3,64,1024]{2,1,0:T(8,128)(2,1)S(1)}, bf16[3,64,1024]{2,1,0:T(8,128)(2,1)S(1)}, u32[]{:S(2)}, u32[]{:S(2)}) collective-permute-start(bf16[3,64,1024]{2,1,0:T(8,128)(2,1)S(1)} %collective-permute-done.9.refs_4_), channel_id=1, source_target_pairs={{4,0},{0,4},{12,8},{8,12},{20,16},{16,20},{28,24},{24,28},{5,1},{1... | collective-permute-start | bytes 1179656 | tf_op jit(solution)/shard_map/ppermute | solution.py:214
  32.5 17.8 %collective-permute-start.8 = (bf16[3,64,1024]{2,1,0:T(8,128)(2,1)S(1)}, bf16[3,64,1024]{2,1,0:T(8,128)(2,1)S(1)}, u32[]{:S(2)}, u32[]{:S(2)}) collective-permute-start(bf16[3,64,1024]{2,1,0:T(8,128)(2,1)S(1)} %collective-permute-done.7.refs_2_), channel_id=1, source_target_pairs={{4,0},{0,4},{12,8},{8,12},{20,16},{16,20},{28,24},{24,28},{5,1},{1... | collective-permute-start | bytes 1179656 | tf_op jit(solution)/shard_map/ppermute | solution.py:214
  32.9 13.9 %collective-permute-start = (bf16[2,512,128]{2,1,0:T(8,128)(2,1)S(1)}, bf16[2,512,128]{2,1,0:T(8,128)(2,1)S(1)}, u32[]{:S(2)}, u32[]{:S(2)}) collective-permute-start(bf16[2,512,128]{2,1,0:T(8,128)(2,1)S(1)} %get-tuple-element.19.kv_ref), channel_id=1, source_target_pairs={{3,0},{2,1},{1,2},{0,3},{7,4},{6,5},{5,6},{4,7},{11,8},{10,9},{9,1... | collective-permute-start | bytes 786440 | tf_op jit(solution)/shard_map/ppermute | solution.py:211
  40.4 10.1 %copy-start = (bf16[512,1024]{1,0:T(8,128)(2,1)S(1)}, bf16[512,1024]{1,0:T(8,128)(2,1)}, u32[]{:S(2)}) copy-start(bf16[512,1024]{1,0:T(8,128)(2,1)} %w_ref.3) | copy-start | bytes 3145732
